TPU v7x, 32 devices: a whole 2x2x4 slice. The times are simulated.
32 devices in a mesh: tile: 8 (over y, x, core), coarse: 4 (over z).
Axes of the slice: x: 2, y: 2, z: 4, core: 2. Of those that a mesh axis runs over, the one named last changes fastest.
Arguments:
- features: bfloat16 [524288, 256], P(('tile', 'coarse')), may hold values from -6 to 6
- weight_in: bfloat16 [256, 256], replicated, may hold values from -0.375 to 0.375
- bias_in: float32 [256], replicated, may hold values from -3 to 3
- weight_mid: bfloat16 [256, 256], replicated, may hold values from -0.375 to 0.375
- bias_mid: float32 [256], replicated, may hold values from -3 to 3
- weight_out: float32 [256], replicated, may hold values from -0.375 to 0.375
- fine_block: int32 [32, 128], P(('tile', 'coarse')), may hold values from 0 to 127, each once within a row
- owner_dev: int32 [4096, 1], P(('tile', 'coarse')), may hold values from 0 to 31; in each aligned block of 128 rows (0 to 127, 128 to 255, ...) at most 8 rows name the same one
- coarse_local: int32 [4096], P(('tile', 'coarse')), may hold values from 0 to 127
- warp_weights: bfloat16 [4096, 128, 64], P(('tile', 'coarse')), may hold values from -0.5 to 0.5
- reference_map: float32 [64, 4096], P(None, ('tile', 'coarse')), may hold values from -6 to 6
- valid_mask: int32 [64, 4096], P(None, ('tile', 'coarse')), may hold values 0 or 1
Outputs:
- coarse_pred: float32 [64, 4096], P(None, ('tile', 'coarse'))
- grad_weight_in: float32 [256, 256], replicated
- grad_bias_in: float32 [256], replicated
- grad_weight_mid: float32 [256, 256], replicated
- grad_bias_mid: float32 [256], replicated
- grad_weight_out: float32 [256], replicated
Inputs may be any that keep to these rules, and one draw needn't show every extreme that they name: `fine_block`: each row lists the device's 128 fine blocks once each. `owner_dev`: among the rows of one device no owner is named more than 8 times; some owner is named exactly 8 times by some device.
All inputs are finite; a program needn't handle non-finite values. No bound on the sum of `valid_mask` on one device may be relied on, other than what follows from the above.
Results may differ from a plain program's by a relative error of at most 0.0043.
Values sent between devices are 32-bit elements; how exact they have to be, the bound alone decides.
No kernel may reach another device: no remote copies, remote signals or barrier semaphores. Data moves between devices by JAX's collectives and lax.ppermute only.
A program may use at most 128 MiB of HBM per device.

v0:
```python
import math

import jax
import jax.numpy as jnp
from jax import lax
from jax.sharding import PartitionSpec as P


def run_head(pixel_feats, weight_in, bias_in, weight_mid, bias_mid, weight_out):
    pre_first = jnp.dot(pixel_feats, weight_in, preferred_element_type=jnp.float32) + bias_in
    act_first = jnp.maximum(pre_first, 0.0).astype(jnp.bfloat16)
    pre_second = jnp.dot(act_first, weight_mid, preferred_element_type=jnp.float32) + bias_mid
    act_second = jnp.maximum(pre_second, 0.0)
    predicted = jnp.dot(act_second, weight_out, precision=lax.Precision.HIGHEST)
    return (pre_first, act_first, pre_second, act_second, predicted)


def shards(
    features,
    weight_in,
    bias_in,
    weight_mid,
    bias_mid,
    weight_out,
    fine_block,
    owner_dev,
    coarse_local,
    warp_weights,
    reference_map,
    valid_mask,
):
    fb_count = warp_weights.shape[0]
    block_pix = warp_weights.shape[1]
    cell_count = warp_weights.shape[2]
    cb_local = reference_map.shape[1]
    devices = lax.axis_size(("tile", "coarse"))
    slot_cap = max(2, 2 * fb_count // devices)
    pre_first, act_first, pre_second, act_second, predicted = run_head(
        features, weight_in, bias_in, weight_mid, bias_mid, weight_out
    )
    block_list = fine_block[0]
    chosen = predicted.reshape(fb_count, block_pix)[block_list]
    warp_float = warp_weights.astype(jnp.float32)
    partial_value = jnp.einsum("kp,kpc->kc", chosen, warp_float, precision=lax.Precision.HIGHEST)
    target = owner_dev[:, 0]
    loss_scale = 1.0 / math.sqrt(fb_count * devices * block_pix)
    valid_float = valid_mask.astype(jnp.float32)
    onehot = (target[:, None] == jnp.arange(devices, dtype=jnp.int32)[None, :]).astype(jnp.int32)
    slot_rank = jnp.sum(jnp.cumsum(onehot, axis=0) * onehot, axis=1) - 1
    send_sums = (
        jnp.zeros((devices, slot_cap, cell_count), jnp.float32)
        .at[target, slot_rank]
        .set(partial_value)
    )
    send_ids = (
        jnp.zeros((devices, slot_cap), jnp.float32)
        .at[target, slot_rank]
        .set(coarse_local.astype(jnp.float32))
    )
    recv_sums, recv_ids = (
        lax.all_to_all(send_sums, ("tile", "coarse"), split_axis=0, concat_axis=0, tiled=True),
        lax.all_to_all(send_ids, ("tile", "coarse"), split_axis=0, concat_axis=0, tiled=True),
    )
    slot_ids = recv_ids.astype(jnp.int32).reshape(-1)
    coarse_pred = (
        jnp.zeros((cell_count, cb_local), jnp.float32)
        .at[:, slot_ids]
        .add(recv_sums.reshape(-1, cell_count).T)
    )
    grad_coarse = loss_scale * valid_float * (coarse_pred - reference_map)
    returning = grad_coarse[:, slot_ids].T.reshape(devices, slot_cap, cell_count)
    returned = lax.all_to_all(
        returning, ("tile", "coarse"), split_axis=0, concat_axis=0, tiled=True
    )
    grad_cols = returned[target, slot_rank]
    grad_blocks = jnp.einsum("kpc,kc->kp", warp_float, grad_cols, precision=lax.Precision.HIGHEST)
    grad_pred = (
        jnp.zeros((fb_count, block_pix), jnp.float32).at[block_list].set(grad_blocks).reshape(-1)
    )
    gw_out = jnp.sum(act_second * grad_pred[:, None], axis=0)
    grad_pre2 = grad_pred[:, None] * weight_out[None, :] * (pre_second > 0).astype(jnp.float32)
    gb_mid = jnp.sum(grad_pre2, axis=0)
    grad_low2 = grad_pre2.astype(jnp.bfloat16)
    gw_mid = lax.dot_general(
        act_first, grad_low2, (((0,), (0,)), ((), ())), preferred_element_type=jnp.float32
    )
    grad_act1 = lax.dot_general(
        grad_low2, weight_mid, (((1,), (1,)), ((), ())), preferred_element_type=jnp.float32
    )
    grad_low1 = (grad_act1 * (pre_first > 0).astype(jnp.float32)).astype(jnp.bfloat16)
    gb_in = jnp.sum(lax.optimization_barrier(grad_low1).astype(jnp.float32), axis=0)
    gw_in = lax.dot_general(
        features, grad_low1, (((0,), (0,)), ((), ())), preferred_element_type=jnp.float32
    )
    totals = lax.psum((gw_in, gb_in, gw_mid, gb_mid, gw_out), ("tile", "coarse"))
    return (coarse_pred, totals[0], totals[1], totals[2], totals[3], totals[4])


def solution(mesh):
    in_specs = (
        P(("tile", "coarse"), None),
        P(),
        P(),
        P(),
        P(),
        P(),
        P(("tile", "coarse"), None),
        P(("tile", "coarse"), None),
        P(("tile", "coarse")),
        P(("tile", "coarse"), None, None),
        P(None, ("tile", "coarse")),
        P(None, ("tile", "coarse")),
    )
    out_specs = (P(None, ("tile", "coarse")), P(), P(), P(), P(), P())
    return jax.shard_map(shards, mesh=mesh, in_specs=in_specs, out_specs=out_specs, check_vma=False)
```

profile of v0, /device:TPU:0, one launch (start us, length us, event | category | flops | bytes accessed | tf_op | source)
XLA Modules:
  0.0 289.8 jit_solution(16880792537017684492)
XLA Ops:
  7.2 0.8 convert_element_type.39
  8.0 0.7 fusion.17
  8.9 0.8 select_reduce_fusion
  9.7 0.7 fusion.23
  10.4 6.4 %scatter_fusion = f32[32,8]{0,1:T(8,128)S(1)} fusion(f32[32,8]{0,1:T(8,128)S(1)} %broadcast_in_dim.9, s32[128]{0:T(128)S(1)} %get-tuple-element.38, f32[128]{0:T(128)S(1)} %convert_element_type.39), kind=kCustom, calls=%fused_computation.3 | custom fusion | bytes 2560 | tf_op jit(solution)/shard_map/scatter | solution.py:58
  16.9 0.7 copy.32
  17.5 7.3 %all-to-all-start = ((f32[32,1,8]{2,1,0:T(1,128)}), f32[32,1,8]{2,1,0:T(1,128)S(1)}, u32[]{:S(2)}, u32[]{:S(2)}) async-start(f32[32,1,8]{2,1,0:T(1,128)} %copy.32), calls=%async_computation | async-start | bytes 32768 | tf_op jit(solution)/shard_map/all_to_all | solution.py:62
  25.6 11.6 %convolution_add_fusion.1 = f32[16384,256]{1,0:T(8,128)} fusion(bf16[16384,256]{1,0:T(8,128)(2,1)} %param.12, bf16[256,256]{1,0:T(8,128)(2,1)} %param.13, f32[256]{0:T(256)} %param.14), kind=kOutput, calls=%fused_computation.8 | convolution fusion | flops 2151677952 | bytes 25297920 | tf_op jit(solution)/shard_map/dot_general | solution.py:10
  37.1 13.8 %convolution_add_fusion = f32[16384,256]{1,0:T(8,128)} fusion(bf16[256,256]{1,0:T(8,128)(2,1)S(1)} %copy-done.1, f32[256]{0:T(256)S(1)} %copy-done.6, f32[16384,256]{1,0:T(8,128)} %convolution_add_fusion.1), kind=kOutput, calls=%fused_computation.7 | convolution fusion | flops 2160066560 | bytes 33686528 | tf_op jit(solution)/shard_map/dot_general | solution.py:12
  51.0 18.1 %fusion.3 = f32[1,16384]{1,0:T(1,128)S(1)} fusion(f32[256,1]{0,1:T(1,128)S(1)} %bitcast.71, f32[16384,256]{1,0:T(8,128)} %convolution_add_fusion), kind=kOutput, calls=%fused_computation.17 | convolution fusion | flops 54525952 | bytes 16843776 | tf_op jit(solution)/shard_map/dot_general | solution.py:14
  69.7 3.3 %fusion.29 = f32[128,1,64]{2,1,0:T(1,128)S(1)} fusion(f32[128,128,1]{1,2,0:T(1,128)S(1)} %bitcast.68, bf16[128,128,64]{1,2,0:T(8,128)(2,1)S(1)} %copy-done), kind=kOutput, calls=%fused_computation.55 | convolution fusion | flops 12582912 | bytes 2195456 | tf_op jit(solution)/shard_map/kp,kpc->kc/dot_general | solution.py:44
  73.1 6.6 %scatter_fusion.1 = f32[32,8,64]{2,1,0:T(8,128)S(1)} fusion(f32[32,8,64]{2,1,0:T(8,128)S(1)} %broadcast_in_dim.10, s32[128]{0:T(128)S(1)} %get-tuple-element.38, f32[128,64]{1,0:T(8,128)S(1)} %bitcast.66), kind=kCustom, calls=%fused_computation.4 | custom fusion | bytes 99328 | tf_op jit(solution)/shard_map/scatter | solution.py:53
  79.6 0.8 reshape.167
  80.4 5.8 %all-to-all-start.1 = ((f32[32,1,512]{2,1,0:T(1,128)}), f32[32,1,512]{2,1,0:T(1,128)S(1)}, u32[]{:S(2)}, u32[]{:S(2)}) async-start(f32[32,1,512]{2,1,0:T(1,128)} %reshape.167), calls=%async_computation.1 | async-start | bytes 131072 | tf_op jit(solution)/shard_map/all_to_all | solution.py:61
  86.5 7.3 %all-to-all-done.1 = f32[32,1,512]{2,1,0:T(1,128)S(1)} async-done(((f32[32,1,512]{2,1,0:T(1,128)}), f32[32,1,512]{2,1,0:T(1,128)S(1)}, u32[]{:S(2)}, u32[]{:S(2)}) %all-to-all-start.1) | async-done | bytes 65568 | tf_op jit(solution)/shard_map/all_to_all | solution.py:61
  94.3 0.8 reduce.4
  95.2 1.8 scatter_custom_fusion.2
  97.2 0.7 gather_fusion.1
  98.1 9.2 %all_to_all.19 = f32[32,1,512]{2,1,0:T(1,128)S(1)} all-to-all(f32[32,1,512]{2,1,0:T(1,128)S(1)} %reshape.169), channel_id=1, replica_groups=mesh['tile'=8,'coarse'=4] {'tile','coarse'}, dimensions={0} | all-to-all | bytes 131072 | tf_op jit(solution)/shard_map/all_to_all | solution.py:72
  107.2 0.8 reduce.5
  108.1 1.0 gather_fusion.2
  109.1 1.7 fusion.30
  110.8 0.9 scatter_custom_fusion.3
  111.7 10.7 %multiply_reduce_fusion = (f32[256]{0:T(256)S(1)}, f32[256]{0:T(256)S(1)}, pred[16384,256]{1,0:T(32,128)(4,1)S(1)}) fusion(f32[16384,256]{1,0:T(8,128)} %convolution_add_fusion, f32[16384]{0:T(1024)S(1)} %bitcast.63, f32[256]{0:T(256)S(1)} %copy-done.5), kind=kLoop, calls=%fused_computation.11 | loop fusion | flops 29359616 | bytes 21040128 | tf_op jit(solution)/shard_map/reduce_sum | solution.py:80
  122.4 11.7 %fusion.5 = f32[256,256]{1,0:T(8,128)} fusion(pred[16384,256]{1,0:T(32,128)(4,1)S(1)} %get-tuple-element.37, f32[256]{0:T(256)S(1)} %copy-done.5, f32[16384]{0:T(1024)S(1)} %bitcast.64, f32[16384,256]{1,0:T(8,128)} %convolution_add_fusion.1), kind=kOutput, calls=%fused_computation.19 | convolution fusion | flops 2168455168 | bytes 21300224 | tf_op jit(solution)/shard_map/dot_general | solution.py:84
  134.1 10.5 %fusion = bf16[16384,256]{1,0:T(8,128)(2,1)} fusion(bf16[256,256]{1,0:T(8,128)(2,1)S(1)} %copy-done.1, f32[16384,256]{1,0:T(8,128)} %convolution_add_fusion.1, pred[16384,256]{1,0:T(32,128)(4,1)S(1)} %get-tuple-element.37, f32[256]{0:T(256)S(1)} %copy-done.5, f32[16384]{0:T(1024)S(1)} %bitcast.65), kind=kOutput, calls=%fused_computation.10 | convolution fusion | flops 2172649472 | bytes 29557760 | tf_op jit(solution)/shard_map/dot_general | solution.py:87
  144.5 8.8 %convolution_bitcast_fusion = f32[256,256]{0,1:T(8,128)} fusion(bf16[16384,256]{1,0:T(8,128)(2,1)} %fusion, bf16[16384,256]{1,0:T(8,128)(2,1)} %param.12), kind=kOutput, calls=%fused_computation.28 | convolution fusion | flops 2147483648 | bytes 17039360 | tf_op jit(solution)/shard_map/dot_general | solution.py:92
  153.4 6.6 %convert_reduce_fusion = f32[256]{0:T(256)S(1)} fusion(bf16[16384,256]{1,0:T(8,128)(2,1)} %fusion), kind=kLoop, calls=%fused_computation.12 | loop fusion | flops 8388352 | bytes 8389632 | tf_op jit(solution)/shard_map/reduce_sum | solution.py:91
  160.0 38.0 %all-reduce = (f32[256]{0:T(256)}, f32[256]{0:T(256)}, f32[256]{0:T(256)}) all-reduce(f32[256]{0:T(256)S(1)} %convert_reduce_fusion, f32[256]{0:T(256)S(1)} %get-tuple-element.31, f32[256]{0:T(256)S(1)} %get-tuple-element.30), channel_id=1, replica_groups=mesh['tile'=8,'coarse'=4] {'tile','coarse'}, use_global_device_ids=true, to_apply=%region_8.9 | all-reduce | flops 768 | bytes 6144 | tf_op jit(solution)/shard_map/psum | solution.py:95
  197.9 81.6 %all-reduce.4.cloned.1.call-done = (f32[256,256]{0,1:T(8,128)}, f32[256,256]{1,0:T(8,128)}) async-done(((f32[256,256]{0,1:T(8,128)}, f32[256,256]{1,0:T(8,128)}), (f32[256,256]{0,1:T(8,128)}, f32[256,256]{1,0:T(8,128)})) %all-reduce.4.cloned.1.call-update) | async-done | bytes 524304 | tf_op jit(solution)/shard_map/psum | solution.py:95
  279.5 1.8 copy.36
  281.3 1.7 copy.48
  (34 shorter events, 2.7 us)
Async XLA Ops:
  7.2 62.5 %copy-start = (bf16[128,128,64]{1,2,0:T(8,128)(2,1)S(1)}, bf16[128,128,64]{1,2,0:T(8,128)(2,1)}, u32[]{:S(2)}) copy-start(bf16[128,128,64]{1,2,0:T(8,128)(2,1)} %param.21) | copy-start | bytes 6291460
  17.5 62.9 %all-to-all-start = ((f32[32,1,8]{2,1,0:T(1,128)}), f32[32,1,8]{2,1,0:T(1,128)S(1)}, u32[]{:S(2)}, u32[]{:S(2)}) async-start(f32[32,1,8]{2,1,0:T(1,128)} %copy.32), calls=%async_computation | async-start | bytes 32768 | tf_op jit(solution)/shard_map/all_to_all | solution.py:62
  25.5 11.6 %copy-start.1 = (bf16[256,256]{1,0:T(8,128)(2,1)S(1)}, bf16[256,256]{1,0:T(8,128)(2,1)}, u32[]{:S(2)}) copy-start(bf16[256,256]{1,0:T(8,128)(2,1)} %param.15) | copy-start | bytes 393220
  25.5 11.6 %copy-start.6 = (f32[256]{0:T(256)S(1)}, f32[256]{0:T(256)}, u32[]{:S(2)}) copy-start(f32[256]{0:T(256)} %param.16) | copy-start | bytes 3076
  37.1 13.9 %copy-start.5 = (f32[256]{0:T(256)S(1)}, f32[256]{0:T(256)}, u32[]{:S(2)}) copy-start(f32[256]{0:T(256)} %param.17) | copy-start | bytes 3076
  51.0 46.1 %copy-start.3 = (f32[64,128]{1,0:T(8,128)S(1)}, f32[64,128]{1,0:T(8,128)}, u32[]{:S(2)}) copy-start(f32[64,128]{1,0:T(8,128)} %param.22) | copy-start | bytes 98308
  51.0 46.1 %copy-start.4 = (s32[64,128]{1,0:T(8,128)S(1)}, s32[64,128]{1,0:T(8,128)}, u32[]{:S(2)}) copy-start(s32[64,128]{1,0:T(8,128)} %param.23) | copy-start | bytes 98308
  80.4 13.3 %all-to-all-start.1 = ((f32[32,1,512]{2,1,0:T(1,128)}), f32[32,1,512]{2,1,0:T(1,128)S(1)}, u32[]{:S(2)}, u32[]{:S(2)}) async-start(f32[32,1,512]{2,1,0:T(1,128)} %reshape.167), calls=%async_computation.1 | async-start | bytes 131072 | tf_op jit(solution)/shard_map/all_to_all | solution.py:61
  86.3 193.2 %all-reduce.4.cloned.1.call-start = ((), (), s32[]{:S(2)}) async-start(), calls=%async_computation.3 | async-start | bytes 1048576 | tf_op jit(solution)/shard_map/psum | solution.py:95
  97.1 37.0 %copy-start.2 = (f32[64,128]{1,0:T(8,128)}, f32[64,128]{1,0:T(8,128)S(1)}, u32[]{:S(2)}) copy-start(f32[64,128]{1,0:T(8,128)S(1)} %copy.35) | copy-start | bytes 98308
Sparse Core Ops, SparseCore 0:
  153.5 125.9 all-reduce.3
where the time goes:
time: 290 us
  waiting for transfers between devices  88.9 us (31%)
  matrix products  79.5 us (27%)
  blocking collectives  47.1 us (16%)
  other arithmetic  24.6 us (8%)
  local copies, waits for them, and re-layouts  22.2 us (8%)
  between operations  14.2 us (5%)
  starting transfers between devices  13.2 us (5%)
    psum x1, waiting for transfers between devices, shards(): lax.psum((gw_in, gb_in, gw_mid, gb_mid, gw_out), ('tile', 'coarse'))  81.6 us
    psum x1, blocking collectives, shards(): lax.psum((gw_in, gb_in, gw_mid, gb_mid, gw_out), ('tile', 'coarse'))  38 us
    dot_general x1, matrix products, run_head(): predicted = jnp.dot(act_second, weight_out, precision=lax.Precision.HIGHEST)  18.1 us
    dot_general x1, matrix products, run_head(): jnp.dot(act_first, weight_mid, preferred_element_type=jnp.float32)  13.8 us
    dot_general x1, matrix products, shards(): lax.dot_general(act_first, grad_low2, (((0,), (0,)), ((), ())), preferred...  11.7 us
    dot_general x1, matrix products, run_head(): jnp.dot(pixel_feats, weight_in, preferred_element_type=jnp.float32)  11.6 us
    reduce_sum x1, other arithmetic, shards(): gw_out = jnp.sum(act_second * grad_pred[:, None], axis=0)  10.7 us
    dot_general x1, matrix products, shards(): lax.dot_general(grad_low2, weight_mid, (((1,), (1,)), ((), ())), preferre...  10.5 us
  transfers between devices with their start and end apart: 3, of which 2 were waited for; matrix products, arithmetic and copies ran while one was open for 21% of the time, Pallas kernels for 0%

commit v1 on v0

v1 whole, which is shorter than its diff:
```python
import functools
import math

import jax
import jax.numpy as jnp
from jax import lax
from jax.experimental import pallas as pl
from jax.experimental.pallas import tpu as pltpu
from jax.sharding import Mesh
from jax.sharding import PartitionSpec as P

ALL = ("chip", "core", "coarse")
CHIPS = ("chip", "coarse")
F32 = jnp.float32
BF16 = jnp.bfloat16
NT = (((1,), (1,)), ((), ()))
NN = (((1,), (0,)), ((), ()))


def dot(a, b, dims=NN):
    return lax.dot_general(a, b, dims, preferred_element_type=F32)


def split3(x):
    hi = x.astype(BF16).astype(F32)
    rest = x - hi
    mid = rest.astype(BF16).astype(F32)
    low = (rest - mid).astype(BF16).astype(F32)
    return hi, mid, low


def terms_by_row(x):
    hi, mid, low = split3(x)
    row = lax.broadcasted_iota(jnp.int32, x.shape, 0)
    return jnp.where(row == 0, hi, jnp.where(row == 1, mid, jnp.where(row == 2, low, 0.0)))


def column(vec, lanes):
    return jnp.broadcast_to(vec, (lanes, vec.shape[1])).T


def head_kernel(
    devices, cap, chunk,
    fine_s, owner_s, local_s,
    feat_r, win_r, bin_r, wmid_r, bmid_r, wout_r, warp_r,
    act1_r, act2_r, send_r, rows_r,
    winT, wmidT, b1, b2, wo, pred8, count_s,
):
    step = pl.program_id(0)
    blocks, cells, pix = warp_r.shape
    tile = feat_r.shape[0]
    per_chunk = chunk // pix

    @pl.when(step == 0)
    def _():
        winT[...] = win_r[...].astype(F32).T.astype(BF16)
        wmidT[...] = wmid_r[...].astype(F32).T.astype(BF16)
        b1[...] = column(bin_r[...], chunk)
        b2[...] = column(bmid_r[...], chunk)
        wo[...] = column(wout_r[...], chunk)
        lane = lax.broadcasted_iota(jnp.int32, send_r.shape, 1)
        send_r[...] = jnp.where(lane < cells, 0.0, -1.0)

        def clear(i, c):
            count_s[i] = 0
            return c

        lax.fori_loop(0, devices, clear, 0)

        def slot(k, c):
            owner = owner_s[k]
            rank = count_s[owner]
            count_s[owner] = rank + 1
            rows_r[k] = owner * cap + rank
            return c

        lax.fori_loop(0, blocks, slot, 0)

    for i in range(tile // chunk):
        here = slice(i * chunk, (i + 1) * chunk)
        pre1 = dot(winT[...], feat_r[here, :], NT) + b1[...]
        act1 = jnp.maximum(pre1, 0.0).astype(BF16)
        act1_r[0, :, here] = act1
        act2 = jnp.maximum(dot(wmidT[...], act1) + b2[...], 0.0)
        act2_r[0, :, here] = act2.astype(BF16)
        pred = jnp.sum(act2 * wo[...], axis=0, keepdims=True)
        for b in range(per_chunk):
            one = jnp.broadcast_to(pred[:, b * pix:(b + 1) * pix], (8, pix))
            pred8[step * (tile // pix) + i * per_chunk + b] = terms_by_row(one)

    @pl.when(step == pl.num_programs(0) - 1)
    def _():
        def entry(k, c):
            part = dot(pred8[fine_s[k]].astype(BF16), warp_r[k], NT)
            part = jnp.sum(part, axis=0, keepdims=True)
            row = rows_r[k]
            send_r[pl.ds(row, 1), 0:cells] = part
            tag = jnp.full((1, send_r.shape[1] - cells), local_s[k], jnp.int32).astype(F32)
            send_r[pl.ds(row, 1), cells:] = tag
            return c

        lax.fori_loop(0, blocks, entry, 0, unroll=8)


def coarse_kernel(scale, recv_r, ref_r, valid_r, cp_r, back_r):
    cells, cb = ref_r.shape
    recv = recv_r[...]
    lane = lax.broadcasted_iota(jnp.int32, recv.shape, 1)
    half = recv.shape[1] // 2
    tag = jnp.where(lane < half, pltpu.roll(recv, half, 1), recv)
    pick = (tag == lane.astype(F32)).astype(F32).astype(BF16)
    vals = recv.T[0:cells, :]
    three = jnp.concatenate([t.astype(BF16) for t in split3(vals)], axis=0)
    sums = dot(three, pick)
    cp = sums[0:cells] + sums[cells:2 * cells] + sums[2 * cells:3 * cells]
    cp_r[...] = cp
    grad = scale * valid_r[...].astype(F32) * (cp - ref_r[...])
    wide = jnp.concatenate([t.astype(BF16) for t in split3(grad)], axis=1)
    wide = jnp.concatenate([wide, jnp.zeros_like(wide)], axis=0)
    back_r[...] = dot(jnp.concatenate([pick, pick, pick], axis=1), wide, NT)


def back_kernel(
    chunk,
    fine_s, rows_s,
    ret_r, warp_r, feat_r, act1_r, act2_r, wmid_r, wout_r,
    out_r,
    wo, grad_s, gl1_s, gl2_s, acc_mid, acc_in, acc_wo, acc_bm, acc_bi,
):
    step = pl.program_id(0)
    blocks, cells, pix = warp_r.shape
    hidden, tile = act1_r.shape[1:]
    per_chunk = chunk // pix

    @pl.when(step == 0)
    def _():
        wo[...] = column(wout_r[...], chunk)
        for acc in (acc_mid, acc_in, acc_wo, acc_bm, acc_bi):
            acc[...] = jnp.zeros_like(acc)

        def entry(k, c):
            row = jnp.broadcast_to(ret_r[pl.ds(rows_s[k], 1), :], (8, ret_r.shape[1]))
            terms = terms_by_row(row)[:, 0:cells].astype(BF16)
            grad = jnp.sum(dot(terms, warp_r[k]), axis=0, keepdims=True)
            grad_s[pl.ds(fine_s[k], 1), :] = grad
            return c

        lax.fori_loop(0, blocks, entry, 0, unroll=8)

    for i in range(tile // chunk):
        here = slice(i * chunk, (i + 1) * chunk)
        first = step * (tile // pix) + i * per_chunk
        grad = jnp.concatenate([grad_s[pl.ds(first + b, 1), :] for b in range(per_chunk)], axis=1)
        act2 = act2_r[0, :, here].astype(F32)
        on = act2 > 0
        gp2 = jnp.where(on, grad * wo[...], 0.0)
        gl2 = gp2.astype(BF16)
        gl2_s[:, here] = gl2
        gwo = act2 * grad
        low1 = jnp.where(act1_r[0, :, here].astype(F32) > 0, dot(wmid_r[...], gl2), 0.0)
        gl1_s[:, here] = low1.astype(BF16)
        for acc, val in ((acc_wo, gwo), (acc_bm, gp2), (acc_bi, low1)):
            total = val[:, 0:pix]
            for b in range(1, per_chunk):
                total = total + val[:, b * pix:(b + 1) * pix]
            acc[...] += total
    acc_mid[...] += dot(act1_r[0], gl2_s[...], NT)
    acc_in[...] += dot(gl1_s[...], feat_r[...])

    @pl.when(step == pl.num_programs(0) - 1)
    def _():
        def as_row(acc):
            return jnp.sum(acc[...].T, axis=0, keepdims=True)

        width = acc_mid.shape[1]
        zero = jnp.zeros((6, width), F32)
        tail_mid = jnp.concatenate([as_row(acc_bm), as_row(acc_wo), zero], axis=0)
        tail_in = jnp.concatenate([as_row(acc_bi), jnp.zeros((1, width), F32), zero], axis=0)
        base = 0
        for acc, tail in ((acc_mid, tail_mid), (acc_in, tail_in)):
            for lanes in range(0, width, 128):
                out_r[base:base + hidden, :] = acc[:, lanes:lanes + 128]
                out_r[base + hidden:base + hidden + 8, :] = tail[:, lanes:lanes + 128]
                base += hidden + 8


def last_kernel(core_s, mine_r, other_r, gwin_r, gbin_r, gwmid_r, gbmid_r, gwout_r):
    hidden = gwmid_r.shape[0]
    first = core_s[0] == 0

    def part(want_first):
        use_mine = jnp.logical_xor(first, not want_first)
        whole = jnp.where(use_mine, mine_r[...], other_r[...])
        pieces, tails = [], []
        for base in range(0, whole.shape[0], hidden + 8):
            pieces.append(whole[base:base + hidden])
            tails.append(whole[base + hidden:base + hidden + 8])
        return jnp.concatenate(pieces, axis=1), jnp.concatenate(tails, axis=1)

    mid, tail = part(True)
    gwmid_r[...] = mid
    gbmid_r[...] = tail[0:1]
    gwout_r[...] = tail[1:2]
    win, tail = part(False)
    gwin_r[...] = win.T
    gbin_r[...] = tail[0:1]


def vmem():
    return pl.BlockSpec(memory_space=pltpu.VMEM)


def smem():
    return pl.BlockSpec(memory_space=pltpu.SMEM)


def fixed(shape):
    return pl.BlockSpec(shape, lambda i: (0,) * len(shape), pipeline_mode=pl.Buffered(1))


def all_to_all(x, axes):
    return lax.all_to_all(x, axes, split_axis=0, concat_axis=0, tiled=True)


def shards(
    features, weight_in, bias_in, weight_mid, bias_mid, weight_out,
    fine_block, owner_dev, coarse_local, warp_weights, reference_map, valid_mask,
):
    blocks, pix, cells = warp_weights.shape
    pixels, chans = features.shape
    hidden = weight_mid.shape[0]
    cb = reference_map.shape[1]
    devices = lax.axis_size(ALL)
    chips = lax.axis_size(CHIPS)
    cap = max(2, 2 * blocks // devices)
    slots = devices * cap
    tile, chunk = 2048, 256
    steps = pixels // tile

    warp = jnp.swapaxes(warp_weights, 1, 2)
    fine = fine_block[0]
    owner = owner_dev[:, 0]
    row = lambda v: v[None, :]

    act1, act2, send, rows = pl.pallas_call(
        functools.partial(head_kernel, devices, cap, chunk),
        grid=(steps,),
        in_specs=[
            smem(), smem(), smem(),
            pl.BlockSpec((tile, chans), lambda i: (i, 0)),
            fixed((chans, hidden)), fixed((1, hidden)), fixed((hidden, hidden)),
            fixed((1, hidden)), fixed((1, hidden)), fixed((blocks, cells, pix)),
        ],
        out_specs=[
            pl.BlockSpec((1, hidden, tile), lambda i: (i, 0, 0)),
            pl.BlockSpec((1, hidden, tile), lambda i: (i, 0, 0)),
            pl.BlockSpec((slots, 2 * cells), lambda i: (0, 0)),
            smem(),
        ],
        out_shape=[
            jax.ShapeDtypeStruct((steps, hidden, tile), BF16),
            jax.ShapeDtypeStruct((steps, hidden, tile), BF16),
            jax.ShapeDtypeStruct((slots, 2 * cells), F32),
            jax.ShapeDtypeStruct((blocks,), jnp.int32),
        ],
        scratch_shapes=[
            pltpu.VMEM((hidden, chans), BF16),
            pltpu.VMEM((hidden, hidden), BF16),
            pltpu.VMEM((hidden, chunk), F32),
            pltpu.VMEM((hidden, chunk), F32),
            pltpu.VMEM((hidden, chunk), F32),
            pltpu.VMEM((blocks, 8, pix), F32),
            pltpu.SMEM((devices,), jnp.int32),
        ],
        name="head",
    )(fine, owner, coarse_local, features, weight_in, row(bias_in), weight_mid, row(bias_mid),
      row(weight_out), warp)

    recv = all_to_all(send.reshape(devices, cap, 2 * cells), ALL).reshape(slots, 2 * cells)

    scale = 1.0 / math.sqrt(blocks * devices * pix)
    coarse_pred, back = pl.pallas_call(
        functools.partial(coarse_kernel, scale),
        in_specs=[vmem()] * 3,
        out_specs=[vmem()] * 2,
        out_shape=[
            jax.ShapeDtypeStruct((cells, cb), F32),
            jax.ShapeDtypeStruct((slots, 2 * cells), F32),
        ],
        name="coarse",
    )(recv, reference_map, valid_mask)

    returned = all_to_all(back.reshape(devices, cap, 2 * cells), ALL).reshape(slots, 2 * cells)

    packed_rows = 2 * (hidden + 8) * (chans // 128)
    packed = pl.pallas_call(
        functools.partial(back_kernel, chunk),
        grid=(steps,),
        in_specs=[
            smem(), smem(),
            fixed((slots, 2 * cells)), fixed((blocks, cells, pix)),
            pl.BlockSpec((tile, chans), lambda i: (i, 0)),
            pl.BlockSpec((1, hidden, tile), lambda i: (i, 0, 0)),
            pl.BlockSpec((1, hidden, tile), lambda i: (i, 0, 0)),
            fixed((hidden, hidden)), fixed((1, hidden)),
        ],
        out_specs=pl.BlockSpec((packed_rows, 128), lambda i: (0, 0)),
        out_shape=jax.ShapeDtypeStruct((packed_rows, 128), F32),
        scratch_shapes=[
            pltpu.VMEM((hidden, chunk), F32),
            pltpu.VMEM((blocks, pix), F32),
            pltpu.VMEM((hidden, tile), BF16),
            pltpu.VMEM((hidden, tile), BF16),
            pltpu.VMEM((hidden, hidden), F32),
            pltpu.VMEM((hidden, chans), F32),
            pltpu.VMEM((hidden, pix), F32),
            pltpu.VMEM((hidden, pix), F32),
            pltpu.VMEM((hidden, pix), F32),
        ],
        name="back",
    )(fine, rows, returned, warp, features, act1, act2, weight_mid, row(weight_out))

    core = lax.axis_index("core")
    run = packed_rows * 128 // 2 // chips
    halves = packed.reshape(2, chips, 1, run)
    swap = [(0, 1), (1, 0)]
    keep = lax.dynamic_index_in_dim(halves, core, 0, False)
    give = lax.dynamic_index_in_dim(halves, 1 - core, 0, False)
    half = keep + lax.ppermute(give, "core", swap)
    share = jnp.sum(all_to_all(half, CHIPS), axis=0)
    mine = all_to_all(jnp.broadcast_to(share[None], (chips, 1, run)), CHIPS)
    other = lax.ppermute(mine, "core", swap)

    flat = lambda x: x.reshape(packed_rows // 2, 128)
    gw_in, gb_in, gw_mid, gb_mid, gw_out = pl.pallas_call(
        last_kernel,
        in_specs=[smem(), vmem(), vmem()],
        out_specs=[vmem()] * 5,
        out_shape=[
            jax.ShapeDtypeStruct((chans, hidden), F32),
            jax.ShapeDtypeStruct((1, hidden), F32),
            jax.ShapeDtypeStruct((hidden, hidden), F32),
            jax.ShapeDtypeStruct((1, hidden), F32),
            jax.ShapeDtypeStruct((1, hidden), F32),
        ],
        name="last",
    )(core.astype(jnp.int32).reshape(1), flat(mine), flat(other))
    return (coarse_pred, gw_in, gb_in[0], gw_mid, gb_mid[0], gw_out[0])


def solution(mesh):
    tile, coarse = mesh.shape["tile"], mesh.shape["coarse"]
    split = Mesh(mesh.devices.reshape(tile // 2, 2, coarse), ALL)
    in_specs = (
        P(ALL, None), P(), P(), P(), P(), P(),
        P(ALL, None), P(ALL, None), P(ALL), P(ALL, None, None), P(None, ALL), P(None, ALL),
    )
    out_specs = (P(None, ALL), P(), P(), P(), P(), P())
    return jax.shard_map(shards, mesh=split, in_specs=in_specs, out_specs=out_specs, check_vma=False)
```

time: 290 us -> 107 us (0.37)
  matrix products: 79.5 us -> 0 us
  waiting for transfers between devices: 88.9 us -> 11.5 us
  Pallas kernels: 0 us -> 44.7 us
  other arithmetic: 24.6 us -> 0.46 us
  local copies, waits for them, and re-layouts: 22.2 us -> 2.88 us
  between operations: 14.2 us -> 0.71 us
  starting transfers between devices: 13.2 us -> 2.65 us
  blocking collectives: 47.1 us -> 42.9 us
    psum x1 -> x0, waiting for transfers between devices: 81.6 us -> none  [shards(): lax.psum((gw_in, gb_in, gw_mid, gb_mid, gw_out), ('tile', 'coarse'))]
    dot_general x8 -> x0, matrix products: 79.5 us -> none  [the longest x1 18.1 us: run_head(): predicted = jnp.dot(act_second, weight_out, precision=lax.Precision.HIGHEST)]
    pallas_call x0 -> x4, Pallas kernels: none -> 44.7 us  [the longest x1 20.7 us: shards(): pl.pallas_call(functools.partial(back_kernel, chunk), grid=(steps,), in_s...]
    psum x1 -> x0, blocking collectives: 38 us -> none  [shards(): lax.psum((gw_in, gb_in, gw_mid, gb_mid, gw_out), ('tile', 'coarse'))]
    all_to_all x1 -> x3, blocking collectives: 9.19 us -> 42.9 us  [all_to_all(): return lax.all_to_all(x, axes, split_axis=0, concat_axis=0, tiled=True)]
    reduce_sum x3 -> x1, other arithmetic: 18.1 us -> 0.17 us  [shards(): share = jnp.sum(all_to_all(half, CHIPS), axis=0)]
    scatter x3 -> x0, local copies, waits for them, and re-layouts: 13.9 us -> none  [the longest x1 6.56 us: shards(): send_sums = jnp.zeros((devices, slot_cap, cell_count), jnp.float32).at[ta...]
    all_to_all x2 -> x1, starting transfers between devices: 13.2 us -> 2.58 us  [all_to_all(): return lax.all_to_all(x, axes, split_axis=0, concat_axis=0, tiled=True)]
  transfers between devices with their start and end apart: 3 -> 3, of which waited for: 2 -> 3; matrix products, arithmetic and copies ran while one was open for 21% -> 0% of each run, Pallas kernels for 0% -> 0%
where the time goes in v1:
time: 107 us; the launch traced here: 106 us
  Pallas kernels  44.7 us (42%)
  blocking collectives  42.9 us (40%)
  waiting for transfers between devices  11.5 us (11%)
  local copies, waits for them, and re-layouts  2.88 us (3%)
  starting transfers between devices  2.65 us (2%)
    all_to_all x3, blocking collectives, all_to_all(): return lax.all_to_all(x, axes, split_axis=0, concat_axis=0, tiled=True)  42.9 us
    pallas_call x1, Pallas kernels, shards(): pl.pallas_call(functools.partial(back_kernel, chunk), grid=(steps,), in_s...  20.7 us
    pallas_call x1, Pallas kernels, shards(): pl.pallas_call(functools.partial(head_kernel, devices, cap, chunk), grid=...  20 us
    all_to_all x1, waiting for transfers between devices, all_to_all(): return lax.all_to_all(x, axes, split_axis=0, concat_axis=0, tiled=True)  8.37 us
    all_to_all x1, starting transfers between devices, all_to_all(): return lax.all_to_all(x, axes, split_axis=0, concat_axis=0, tiled=True)  2.58 us
  transfers between devices with their start and end apart: 3, of which 3 were waited for; matrix products, arithmetic and copies ran while one was open for 0% of the time, Pallas kernels for 0%

profile of v1, /device:TPU:0, one launch (start us, length us, event | category | flops | bytes accessed | tf_op | source)
XLA Modules:
  0.0 105.8 jit_solution(17770987288408707993)
XLA Ops:
  0.6 20.0 %head.1 = (bf16[8,256,2048]{2,1,0:T(8,128)(2,1)}, bf16[8,256,2048]{2,1,0:T(8,128)(2,1)}, f32[256,128]{1,0:T(8,128)}, s32[128]{0:T(128)}) custom-call(s32[128]{0:T(128)} %bitcast.32, s32[128]{0:T(128)} %bitcast.36, s32[128]{0:T(128)} %local_s.1, bf16[16384,256]{1,0:T(8,128)(2,1)} %feat_r.3, bf16[256,256]{1,0:T(8,128)(2,1)} %win_r.1, f32[1,256]{1,0:T(1,128)} %bitcast.34, ...), custom_call_target="tpu_custom_call" | custom-call | tf_op jit(solution)/shard_map/head/pallas_call | solution.py:245
  20.6 15.8 %all_to_all.20 = f32[32,8,128]{2,1,0:T(8,128)} all-to-all(f32[32,8,128]{2,1,0:T(8,128)} %bitcast.29), channel_id=1, replica_groups=mesh['chip'=4,'core'=2,'coarse'=4] {'chip','core','coarse'}, dimensions={0} | all-to-all | bytes 262144 | tf_op jit(solution)/shard_map/all_to_all | solution.py:222
  36.5 2.1 %coarse.1 = (f32[64,128]{1,0:T(8,128)}, f32[256,128]{1,0:T(8,128)}) custom-call(f32[256,128]{1,0:T(8,128)} %bitcast.26, f32[64,128]{1,0:T(8,128)} %ref_r.1, s32[64,128]{1,0:T(8,128)} %valid_r.1), custom_call_target="tpu_custom_call" | custom-call | tf_op jit(solution)/shard_map/coarse/pallas_call | solution.py:282
  38.6 2.6 %all-to-all-start.1 = ((f32[32,8,128]{2,1,0:T(8,128)}), f32[32,8,128]{2,1,0:T(8,128)S(1)}, u32[]{:S(2)}, u32[]{:S(2)}) async-start(f32[32,8,128]{2,1,0:T(8,128)} %bitcast.28), calls=%async_computation.1 | async-start | bytes 262144 | tf_op jit(solution)/shard_map/all_to_all | solution.py:222
  41.2 8.4 %all-to-all-done.1 = f32[32,8,128]{2,1,0:T(8,128)S(1)} async-done(((f32[32,8,128]{2,1,0:T(8,128)}), f32[32,8,128]{2,1,0:T(8,128)S(1)}, u32[]{:S(2)}, u32[]{:S(2)}) %all-to-all-start.1) | async-done | bytes 131104 | tf_op jit(solution)/shard_map/all_to_all | solution.py:222
  49.5 0.0 copy-start.1
  49.5 0.7 copy-done.1
  50.2 20.7 %back.1 = f32[1056,128]{1,0:T(8,128)} custom-call(s32[128]{0:T(128)} %bitcast.33, s32[128]{0:T(128)} %get-tuple-element.19.rows_s, f32[256,128]{1,0:T(8,128)} %bitcast.25, bf16[128,64,128]{2,1,0:T(8,128)(2,1)} %bitcast.23, bf16[16384,256]{1,0:T(8,128)(2,1)} %feat_r.3, bf16[8,256,2048]{2,1,0:T(8,128)(2,1)} %get-tuple-element.21.act1_r, ...), custom_call_target="tpu_custom_call" | custom-call | tf_op jit(solution)/shard_map/back/pallas_call | solution.py:296
  70.9 1.1 %reshape.46 = f32[2,16,1,4224]{3,1,0,2:T(8,128)S(1)} reshape(f32[1056,128]{1,0:T(8,128)} %back.1) | data formatting | bytes 1081344 | tf_op jit(solution)/shard_map/reshape | solution.py:325
  72.1 0.2 squeeze.25
  72.3 0.1 collective-permute-start
  72.4 1.5 %collective-permute-done = f32[16,1,4224]{2,1,0:T(1,128)S(1)} collective-permute-done((f32[16,1,4224]{2,1,0:T(1,128)S(1)}, f32[16,1,4224]{2,1,0:T(1,128)S(1)}, u32[]{:S(2)}, u32[]{:S(2)}) %collective-permute-start) | collective-permute-done | bytes 270368 | tf_op jit(solution)/shard_map/ppermute | solution.py:329
  73.9 0.3 reshape_add_fusion
  74.2 13.9 %all_to_all.21 = f32[16,1,4224]{2,1,0:T(1,128)S(1)} all-to-all(f32[16,1,4224]{2,1,0:T(1,128)S(1)} %reshape_add_fusion), channel_id=1, replica_groups=mesh['chip'=4,'core'=2,'coarse'=4] {'chip','coarse'}, dimensions={0} | all-to-all | bytes 540672 | tf_op jit(solution)/shard_map/all_to_all | solution.py:222
  88.1 0.2 reduce_sum.9
  88.3 0.1 broadcast_in_dim.19
  88.5 13.2 %all_to_all.22 = f32[16,1,4224]{2,1,0:T(1,128)S(1)} all-to-all(f32[16,1,4224]{2,1,0:T(1,128)S(1)} %broadcast_in_dim.19), channel_id=1, replica_groups=mesh['chip'=4,'core'=2,'coarse'=4] {'chip','coarse'}, dimensions={0} | all-to-all | bytes 540672 | tf_op jit(solution)/shard_map/all_to_all | solution.py:222
  101.6 0.0 copy-start
  101.6 0.0 collective-permute-start.1
  101.7 1.5 %collective-permute-done.1 = f32[16,1,4224]{2,1,0:T(1,128)S(1)} collective-permute-done((f32[16,1,4224]{2,1,0:T(1,128)S(1)}, f32[16,1,4224]{2,1,0:T(1,128)S(1)}, u32[]{:S(2)}, u32[]{:S(2)}) %collective-permute-start.1) | collective-permute-done | bytes 270368 | tf_op jit(solution)/shard_map/ppermute | solution.py:332
  103.2 0.0 copy-start.2
  103.2 0.0 copy-done
  103.2 0.7 copy-done.2
  103.9 1.9 %last.1 = (f32[256,256]{1,0:T(8,128)}, f32[1,256]{1,0:T(1,128)}, f32[256,256]{1,0:T(8,128)}, f32[1,256]{1,0:T(1,128)}, f32[1,256]{1,0:T(1,128)}) custom-call(s32[1]{0:T(128)} %bitcast.8.core_s, f32[528,128]{1,0:T(8,128)} %bitcast.24, f32[528,128]{1,0:T(8,128)} %bitcast.27), custom_call_target="tpu_custom_call" | custom-call | tf_op jit(solution)/shard_map/last/pallas_call | solution.py:335
  (1 shorter events, 0.0 us)
Async XLA Ops:
  38.6 11.0 %all-to-all-start.1 = ((f32[32,8,128]{2,1,0:T(8,128)}), f32[32,8,128]{2,1,0:T(8,128)S(1)}, u32[]{:S(2)}, u32[]{:S(2)}) async-start(f32[32,8,128]{2,1,0:T(8,128)} %bitcast.28), calls=%async_computation.1 | async-start | bytes 262144 | tf_op jit(solution)/shard_map/all_to_all | solution.py:222
  49.5 0.7 copy-start.1
  72.3 1.6 %collective-permute-start = (f32[16,1,4224]{2,1,0:T(1,128)S(1)}, f32[16,1,4224]{2,1,0:T(1,128)S(1)}, u32[]{:S(2)}, u32[]{:S(2)}) collective-permute-start(f32[16,1,4224]{2,1,0:T(1,128)S(1)} %squeeze.25), channel_id=1, source_target_pairs={{0,4},{4,0},{1,5},{5,1},{2,6},{6,2},{3,7},{7,3},{8,12},{12,8},{9,1... | collective-permute-start | bytes 811016 | tf_op jit(solution)/shard_map/ppermute | solution.py:329
  101.6 1.6 %copy-start = (f32[16,1,4224]{2,1,0:T(1,128)}, f32[16,1,4224]{2,1,0:T(1,128)S(1)}, u32[]{:S(2)}) copy-start(f32[16,1,4224]{2,1,0:T(1,128)S(1)} %all_to_all.22) | copy-start | bytes 811012
  101.6 1.5 %collective-permute-start.1 = (f32[16,1,4224]{2,1,0:T(1,128)S(1)}, f32[16,1,4224]{2,1,0:T(1,128)S(1)}, u32[]{:S(2)}, u32[]{:S(2)}) collective-permute-start(f32[16,1,4224]{2,1,0:T(1,128)S(1)} %all_to_all.22), channel_id=1, source_target_pairs={{0,4},{4,0},{1,5},{5,1},{2,6},{6,2},{3,7},{7,3},{8,12},{12,8},{9,1... | collective-permute-start | bytes 811016 | tf_op jit(solution)/shard_map/ppermute | solution.py:332
  103.2 0.7 copy-start.2

commit v2 on v1

v2 whole, which is shorter than its diff:
```python
import functools
import math

import jax
import jax.numpy as jnp
from jax import lax
from jax.experimental import pallas as pl
from jax.experimental.pallas import tpu as pltpu
from jax.sharding import Mesh
from jax.sharding import PartitionSpec as P

ALL = ("chip", "core", "coarse")
CHIPS = ("chip", "coarse")
F32 = jnp.float32
BF16 = jnp.bfloat16
NT = (((1,), (1,)), ((), ()))
NN = (((1,), (0,)), ((), ()))


def dot(a, b, dims=NN):
    return lax.dot_general(a, b, dims, preferred_element_type=F32)


def split3(x):
    hi = x.astype(BF16).astype(F32)
    rest = x - hi
    mid = rest.astype(BF16).astype(F32)
    low = (rest - mid).astype(BF16).astype(F32)
    return hi, mid, low


def terms_by_row(x):
    hi, mid, low = split3(x)
    row = lax.broadcasted_iota(jnp.int32, x.shape, 0)
    return jnp.where(row == 0, hi, jnp.where(row == 1, mid, jnp.where(row == 2, low, 0.0)))


def column(vec, lanes):
    return jnp.broadcast_to(vec, (lanes, vec.shape[1])).T


def widen(col, lanes):
    return jnp.concatenate([col] * (lanes // col.shape[1]), axis=1)


def head_kernel(
    devices, cap, chunk,
    fine_s, owner_s, local_s,
    feat_h, win_r, bin_r, wmid_r, bmid_r, wout_r, warp_r,
    act1_h, act2_h, send_r, rows_r, inv_r,
    feat_v, act1_v, act2_v, winT, wmidT, b1, b2, wo, part_s, count_s, sem_in, sem_out,
):
    blocks, cells, pix = warp_r.shape
    steps, tile = feat_v.shape[:2]
    per_chunk, per_step = chunk // pix, tile // pix

    def load(step):
        rows = pl.ds(pl.multiple_of(step * tile, tile), tile)
        return pltpu.make_async_copy(feat_h.at[rows], feat_v.at[step], sem_in.at[step])

    def stores(step):
        return [
            pltpu.make_async_copy(src.at[step], dst.at[step], sem_out.at[n, step])
            for n, (src, dst) in enumerate(((act1_v, act1_h), (act2_v, act2_h)))
        ]

    for step in range(steps):
        load(step).start()

    def prepare():
        winT[...] = win_r[...].astype(F32).T.astype(BF16)
        wmidT[...] = wmid_r[...].astype(F32).T.astype(BF16)
        b1[...] = column(bin_r[...], pix)
        b2[...] = column(bmid_r[...], pix)
        wo[...] = column(wout_r[...], pix)
        lane = lax.broadcasted_iota(jnp.int32, send_r.shape, 1)
        send_r[...] = jnp.where(lane < cells, 0.0, -1.0)
        for i in range(devices):
            count_s[i] = 0

        def invert(k, c):
            inv_r[fine_s[k]] = k
            return c

        lax.fori_loop(0, blocks, invert, 0, unroll=16)

    prepare()
    lax.fori_loop(0, steps, functools.partial(
        head_step, chunk, per_chunk, per_step, cap, load, stores,
        fine_s, owner_s, local_s, feat_v, act1_v, act2_v, warp_r,
        rows_r, inv_r, winT, wmidT, b1, b2, wo, part_s, count_s), 0)

    def place(k, c):
        send_r[pl.ds(rows_r[k], 1), :] = part_s[pl.ds(k, 1), :]
        return c

    lax.fori_loop(0, blocks, place, 0, unroll=16)
    for step in range(steps):
        for copy in stores(step):
            copy.wait()


def head_step(
    chunk, per_chunk, per_step, cap, load, stores,
    fine_s, owner_s, local_s, feat_v, act1_v, act2_v, warp_r,
    rows_r, inv_r, winT, wmidT, b1, b2, wo, part_s, count_s,
    step, carry,
):
    cells, pix = warp_r.shape[1:]
    tile = feat_v.shape[1]
    load(step).wait()
    feat_r, act1_r, act2_r = feat_v.at[step], act1_v.at[step], act2_v.at[step]

    for q in range(per_step):
        k = step * per_step + q
        owner = owner_s[k]
        rank = count_s[owner]
        count_s[owner] = rank + 1
        rows_r[k] = owner * cap + rank

    count = tile // chunk
    first, preds = {}, {}
    for i in range(count + 2):
        if i < count:
            here = slice(i * chunk, (i + 1) * chunk)
            pre1 = dot(winT[...], feat_r[here, :], NT) + widen(b1[...], chunk)
            first[i] = jnp.maximum(pre1.astype(BF16), jnp.zeros((), BF16))
            act1_r[:, here] = first[i]
        if 0 <= i - 1 < count:
            here = slice((i - 1) * chunk, i * chunk)
            pre2 = dot(wmidT[...], first.pop(i - 1)) + widen(b2[...], chunk)
            act2_r[:, here] = pre2.astype(BF16)
            kept = jnp.maximum(pre2, 0.0) * widen(wo[...], chunk)
            preds[i - 1] = jnp.sum(kept, axis=0, keepdims=True)
        if i >= 2:
            pred = preds.pop(i - 2)
            for b in range(per_chunk):
                k = inv_r[step * per_step + (i - 2) * per_chunk + b]
                one = jnp.broadcast_to(pred[:, b * pix:(b + 1) * pix], (8, pix))
                part = dot(terms_by_row(one).astype(BF16), warp_r[k], NT)
                part_s[pl.ds(k, 1), 0:cells] = jnp.sum(part, axis=0, keepdims=True)
                tag = jnp.full((1, part_s.shape[1] - cells), local_s[k], jnp.int32).astype(F32)
                part_s[pl.ds(k, 1), cells:] = tag

    for copy in stores(step):
        copy.start()
    return carry


def gate_kernel(begin, *refs):
    act1_h, act2_h, wmid_r, wout_r = refs[:4]
    unit_h, token_r, act1_v, act2_v, unit_v, mixed, sem_in, sem_out = refs[-8:]
    count = unit_v.shape[0]

    def loads(i):
        return [
            pltpu.make_async_copy(src.at[begin + i], dst.at[i], sem_in.at[n, i])
            for n, (src, dst) in enumerate(((act2_h, act2_v), (act1_h, act1_v)))
        ]

    def store(i):
        return pltpu.make_async_copy(unit_v.at[i], unit_h.at[begin + i], sem_out.at[i])

    for i in range(count):
        for copy in loads(i):
            copy.start()
    mixed[...] = (wmid_r[...].astype(F32) * wout_r[...]).astype(BF16)
    token_r[...] = jnp.zeros_like(token_r)

    def one(i, carry):
        for copy in loads(i):
            copy.wait()
        for at in range(0, act2_v.shape[2], 256):
            here = slice(at, at + 256)
            on = act2_v[i, :, here] > 0
            mask = jnp.where(on, jnp.ones((), BF16), jnp.zeros((), BF16))
            unit = dot(mixed[...], mask).astype(BF16)
            unit_v[i, :, here] = jnp.where(act1_v[i, :, here] > 0, unit, jnp.zeros((), BF16))
        store(i).start()
        return carry

    lax.fori_loop(0, count, one, 0)
    for i in range(count):
        store(i).wait()


def coarse_kernel(scale, recv_r, ref_r, valid_r, token_r, cp_r, back_r):
    cells, cb = ref_r.shape
    recv = recv_r[...]
    lane = lax.broadcasted_iota(jnp.int32, recv.shape, 1)
    half = recv.shape[1] // 2
    tag = jnp.where(lane < half, pltpu.roll(recv, half, 1), recv)
    pick = (tag == lane.astype(F32)).astype(F32).astype(BF16)
    vals = recv.T[0:cells, :]
    three = jnp.concatenate([t.astype(BF16) for t in split3(vals)], axis=0)
    sums = dot(three, pick)
    cp = sums[0:cells] + sums[cells:2 * cells] + sums[2 * cells:3 * cells]
    cp_r[...] = cp
    grad = scale * valid_r[...].astype(F32) * (cp - ref_r[...])
    wide = jnp.concatenate([t.astype(BF16) for t in split3(grad)], axis=1)
    wide = jnp.concatenate([wide, jnp.zeros_like(wide)], axis=0)
    back_r[...] = dot(jnp.concatenate([pick, pick, pick], axis=1), wide, NT)


def back_kernel(
    chunk,
    rows_s, inv_s,
    core_s, ret_r, warp_r, feat_h, act1_h, act2_h, unit_h,
    keep_r, give_r,
    feat_v, act1_v, act2_v, unit_v, grad_s, gated_s, low1_s, acc_mid, acc_in, acc_bi, sem,
):
    blocks, cells, pix = warp_r.shape
    steps, hidden, tile = act1_v.shape
    per_chunk, per_step = chunk // pix, tile // pix

    def loads(step):
        rows = pl.ds(pl.multiple_of(step * tile, tile), tile)
        pairs = ((act2_h.at[step], act2_v), (act1_h.at[step], act1_v),
                 (unit_h.at[step], unit_v), (feat_h.at[rows], feat_v))
        return [
            pltpu.make_async_copy(src, dst.at[step], sem.at[n, step])
            for n, (src, dst) in enumerate(pairs)
        ]

    for step in range(steps):
        for copy in loads(step):
            copy.start()

    def entry(of_step, q):
        k = inv_s[jnp.minimum(of_step * per_step + q, blocks - 1)]
        row = jnp.broadcast_to(ret_r[pl.ds(rows_s[k], 1), :], (8, ret_r.shape[1]))
        terms = terms_by_row(row)[:, 0:cells].astype(BF16)
        grad_s[q:q + 1, :] = jnp.sum(dot(terms, warp_r[k]), axis=0, keepdims=True)

    for acc in (acc_mid, acc_in, acc_bi):
        acc[...] = jnp.zeros_like(acc)
    for q in range(per_step):
        entry(0, q)

    def one(step, carry):
        for copy in loads(step):
            copy.wait()
        grads = grad_s[...]

        def scale(i):
            here = slice(i * chunk, (i + 1) * chunk)
            first = i * per_chunk
            grad = jnp.concatenate(
                [grads[first + b:first + b + 1] for b in range(per_chunk)], axis=1)
            short = jnp.broadcast_to(grad.astype(BF16), (hidden, chunk))
            gated_s[:, here] = jnp.where(act2_v[step, :, here] > 0, short, jnp.zeros((), BF16))
            low1_s[:, here] = (unit_v[step, :, here].astype(F32) * grad).astype(BF16)

        def gather(i):
            here = slice(i * chunk, (i + 1) * chunk)
            ones = jnp.ones((16, chunk), BF16)
            lhs = jnp.concatenate([act1_v[step, :, here], ones], axis=0)
            acc_mid[...] += dot(lhs, gated_s[:, here], NT)
            acc_in[...] += dot(low1_s[:, here], feat_v[step, here, :])
            acc_bi[...] += dot(ones, low1_s[:, here], NT)

        count = tile // chunk
        scale(0)
        for i in range(count):
            for b in range(per_chunk):
                entry(step + 1, i * per_chunk + b)
            if i + 1 < count:
                scale(i + 1)
            gather(i)
        return carry

    lax.fori_loop(0, steps, one, 0)

    width = acc_mid.shape[1]
    first = core_s[0] == 0
    halves = ((acc_mid, acc_mid[hidden:hidden + 8, :]), (acc_in, acc_bi[0:8, :]))
    for n, (acc, tail) in enumerate(halves):
        mine = first if n == 0 else jnp.logical_not(first)
        for out, chosen in ((keep_r, mine), (give_r, jnp.logical_not(mine))):
            @pl.when(chosen)
            def _(acc=acc, tail=tail, out=out):
                base = 0
                for lanes in range(0, width, 128):
                    out[base:base + hidden, :] = acc[0:hidden, lanes:lanes + 128]
                    out[base + hidden:base + hidden + 8, :] = tail[:, lanes:lanes + 128]
                    base += hidden + 8


def last_kernel(
    core_s, mine_r, other_r, wmid_r, bmid_r, wout_r,
    gwin_r, gbin_r, gwmid_r, gbmid_r, gwout_r,
):
    hidden = gwmid_r.shape[0]
    first = core_s[0] == 0

    def part(want_first):
        use_mine = jnp.logical_xor(first, not want_first)
        whole = jnp.where(use_mine, mine_r[...], other_r[...])
        pieces, tails = [], []
        for base in range(0, whole.shape[0], hidden + 8):
            pieces.append(whole[base:base + hidden])
            tails.append(whole[base + hidden:base + hidden + 8])
        return jnp.concatenate(pieces, axis=1), jnp.concatenate(tails, axis=1)

    gated, tail = part(True)
    count = tail[0:1]
    gwmid_r[...] = gated * wout_r[...]
    gbmid_r[...] = count * wout_r[...]
    through = jnp.sum(gated * wmid_r[...].astype(F32), axis=0, keepdims=True)
    gwout_r[...] = through + bmid_r[...] * count
    win, tail = part(False)
    gwin_r[...] = win.T
    gbin_r[...] = tail[0:1]


def vmem():
    return pl.BlockSpec(memory_space=pltpu.VMEM)


def smem():
    return pl.BlockSpec(memory_space=pltpu.SMEM)


def limit(mebibytes):
    return pltpu.CompilerParams(vmem_limit_bytes=mebibytes << 20)


def hbm():
    return pl.BlockSpec(memory_space=pl.ANY)


def all_to_all(x, axes):
    return lax.all_to_all(x, axes, split_axis=0, concat_axis=0, tiled=True)


def shards(
    features, weight_in, bias_in, weight_mid, bias_mid, weight_out,
    fine_block, owner_dev, coarse_local, warp_weights, reference_map, valid_mask,
):
    blocks, pix, cells = warp_weights.shape
    pixels, chans = features.shape
    hidden = weight_mid.shape[0]
    cb = reference_map.shape[1]
    devices = lax.axis_size(ALL)
    chips = lax.axis_size(CHIPS)
    cap = max(2, 2 * blocks // devices)
    slots = devices * cap
    tile, chunk = 2048, 512
    steps = pixels // tile

    warp = jnp.swapaxes(warp_weights, 1, 2)
    fine = fine_block[0]
    owner = owner_dev[:, 0]
    row = lambda v: v[None, :]

    act_shape = jax.ShapeDtypeStruct((steps, hidden, tile), BF16)
    act_v = pltpu.VMEM((steps, hidden, tile), BF16)
    feat_v = pltpu.VMEM((steps, tile, chans), BF16)
    act1, act2, send, rows, inv = pl.pallas_call(
        functools.partial(head_kernel, devices, cap, chunk),
        in_specs=[smem()] * 3 + [hbm()] + [vmem()] * 6,
        out_specs=[hbm(), hbm(), vmem(), smem(), smem()],
        out_shape=[
            act_shape, act_shape,
            jax.ShapeDtypeStruct((slots, 2 * cells), F32),
            jax.ShapeDtypeStruct((blocks,), jnp.int32),
            jax.ShapeDtypeStruct((blocks,), jnp.int32),
        ],
        scratch_shapes=[
            feat_v, act_v, act_v,
            pltpu.VMEM((hidden, chans), BF16),
            pltpu.VMEM((hidden, hidden), BF16),
            pltpu.VMEM((hidden, pix), F32),
            pltpu.VMEM((hidden, pix), F32),
            pltpu.VMEM((hidden, pix), F32),
            pltpu.VMEM((blocks, 2 * cells), F32),
            pltpu.SMEM((devices,), jnp.int32),
            pltpu.SemaphoreType.DMA((steps,)),
            pltpu.SemaphoreType.DMA((2, steps)),
        ],
        compiler_params=limit(58),
        name="head",
    )(fine, owner, coarse_local, features, weight_in, row(bias_in), weight_mid, row(bias_mid),
      row(weight_out), warp)

    def unit_part(begin, count, *after):
        part_v = pltpu.VMEM((count, hidden, tile), BF16)
        return pl.pallas_call(
            functools.partial(gate_kernel, begin),
            in_specs=[hbm(), hbm(), vmem(), vmem()] + [hbm()] * len(after),
            out_specs=[hbm(), vmem()],
            out_shape=[act_shape, jax.ShapeDtypeStruct((8, 128), F32)],
            scratch_shapes=[
                part_v, part_v, part_v,
                pltpu.VMEM((hidden, hidden), BF16),
                pltpu.SemaphoreType.DMA((2, count)),
                pltpu.SemaphoreType.DMA((count,)),
            ],
            input_output_aliases={4: 0} if after else {},
            compiler_params=limit(58),
            cost_estimate=pl.CostEstimate(
                flops=2 * hidden * hidden * tile * count,
                bytes_accessed=6 * hidden * tile * count,
                transcendentals=0,
            ),
            name="gate",
        )(act1, act2, weight_mid, row(weight_out), *after)

    unit, token = unit_part(0, steps // 2)

    recv = all_to_all(send.reshape(devices, cap, 2 * cells), ALL).reshape(slots, 2 * cells)

    scale = 1.0 / math.sqrt(blocks * devices * pix)
    coarse_pred, back = pl.pallas_call(
        functools.partial(coarse_kernel, scale),
        in_specs=[vmem()] * 4,
        out_specs=[vmem()] * 2,
        out_shape=[
            jax.ShapeDtypeStruct((cells, cb), F32),
            jax.ShapeDtypeStruct((slots, 2 * cells), F32),
        ],
        compiler_params=limit(4),
        name="coarse",
    )(recv, reference_map, valid_mask, token)

    unit, _ = unit_part(steps // 2, steps - steps // 2, unit, back)
    returned = all_to_all(back.reshape(devices, cap, 2 * cells), ALL).reshape(slots, 2 * cells)

    half_rows = (hidden + 8) * (chans // 128)
    half_shape = jax.ShapeDtypeStruct((half_rows, 128), F32)
    core = lax.axis_index("core").astype(jnp.int32).reshape(1)
    keep, give = pl.pallas_call(
        functools.partial(back_kernel, chunk),
        in_specs=[smem()] * 3 + [vmem(), vmem()] + [hbm()] * 4,
        out_specs=[vmem(), vmem()],
        out_shape=[half_shape, half_shape],
        scratch_shapes=[
            feat_v, act_v, act_v, act_v,
            pltpu.VMEM((tile // pix, pix), F32),
            pltpu.VMEM((hidden, tile), BF16),
            pltpu.VMEM((hidden, tile), BF16),
            pltpu.VMEM((hidden + 16, hidden), F32),
            pltpu.VMEM((hidden, chans), F32),
            pltpu.VMEM((16, hidden), F32),
            pltpu.SemaphoreType.DMA((4, steps)),
        ],
        compiler_params=limit(58),
        name="back",
    )(rows, inv, core, returned, warp, features, act1, act2, unit)

    run = half_rows * 128 // chips
    swap = [(0, 1), (1, 0)]
    half = keep.reshape(chips, 1, run) + lax.ppermute(give.reshape(chips, 1, run), "core", swap)
    share = jnp.sum(all_to_all(half, CHIPS), axis=0)
    mine = all_to_all(jnp.broadcast_to(share[None], (chips, 1, run)), CHIPS)
    other = lax.ppermute(mine, "core", swap)

    flat = lambda x: x.reshape(half_rows, 128)
    gw_in, gb_in, gw_mid, gb_mid, gw_out = pl.pallas_call(
        last_kernel,
        in_specs=[smem()] + [vmem()] * 5,
        out_specs=[vmem()] * 5,
        out_shape=[
            jax.ShapeDtypeStruct((chans, hidden), F32),
            jax.ShapeDtypeStruct((1, hidden), F32),
            jax.ShapeDtypeStruct((hidden, hidden), F32),
            jax.ShapeDtypeStruct((1, hidden), F32),
            jax.ShapeDtypeStruct((1, hidden), F32),
        ],
        compiler_params=limit(8),
        name="last",
    )(core, flat(mine), flat(other), weight_mid, row(bias_mid),
      row(weight_out))
    return (coarse_pred, gw_in, gb_in[0], gw_mid, gb_mid[0], gw_out[0])


def solution(mesh):
    tile, coarse = mesh.shape["tile"], mesh.shape["coarse"]
    split = Mesh(mesh.devices.reshape(tile // 2, 2, coarse), ALL)
    in_specs = (
        P(ALL, None), P(), P(), P(), P(), P(),
        P(ALL, None), P(ALL, None), P(ALL), P(ALL, None, None), P(None, ALL), P(None, ALL),
    )
    out_specs = (P(None, ALL), P(), P(), P(), P(), P())
    return jax.shard_map(shards, mesh=split, in_specs=in_specs, out_specs=out_specs, check_vma=False)
```

time: 107 us -> 97.5 us (0.911)
  blocking collectives: 42.9 us -> 29.6 us
  starting transfers between devices: 2.65 us -> 12.2 us
  waiting for transfers between devices: 11.5 us -> 5.46 us
  local copies, waits for them, and re-layouts: 2.88 us -> 1.51 us
  other arithmetic: 0.46 us -> 1.68 us
  Pallas kernels: 44.7 us -> 45.9 us
    all_to_all x3 -> x2, blocking collectives: 42.9 us -> 29.6 us  [all_to_all(): return lax.all_to_all(x, axes, split_axis=0, concat_axis=0, tiled=True)]
    all_to_all x1 -> x2, starting transfers between devices: 2.58 us -> 12.1 us  [all_to_all(): return lax.all_to_all(x, axes, split_axis=0, concat_axis=0, tiled=True)]
    all_to_all x1 -> x2, waiting for transfers between devices: 8.37 us -> 2.17 us  [all_to_all(): return lax.all_to_all(x, axes, split_axis=0, concat_axis=0, tiled=True)]
    pallas_call x3 -> x5, Pallas kernels: 42.6 us -> 44.7 us  [the longest x1 14.7 us: shards(): pl.pallas_call(functools.partial(back_kernel, chunk), in_specs=[smem()] *...]
    add x1, other arithmetic: 0.29 us -> 1.51 us  [shards(): keep.reshape(chips, 1, run)]
    reshape x1 -> x0, local copies, waits for them, and re-layouts: 1.14 us -> none  [shards(): halves = packed.reshape(2, chips, 1, run)]
  transfers between devices with their start and end apart: 3 -> 4, of which waited for: 3 -> 4; matrix products, arithmetic and copies ran while one was open for 0% -> 0% of each run, Pallas kernels for 0% -> 15%
where the time goes in v2:
time: 97.5 us; the launch traced here: 97.1 us
  Pallas kernels  45.9 us (47%)
  blocking collectives  29.6 us (30%)
  starting transfers between devices  12.2 us (13%)
  waiting for transfers between devices  5.46 us (6%)
  other arithmetic  1.68 us (2%)
  local copies, waits for them, and re-layouts  1.51 us (2%)
    all_to_all x2, blocking collectives, all_to_all(): return lax.all_to_all(x, axes, split_axis=0, concat_axis=0, tiled=True)  29.6 us
    pallas_call x1, Pallas kernels, shards(): pl.pallas_call(functools.partial(back_kernel, chunk), in_specs=[smem()] *...  14.7 us
    pallas_call x1, Pallas kernels, shards(): pl.pallas_call(functools.partial(head_kernel, devices, cap, chunk), in_sp...  14.6 us
    pallas_call x2, Pallas kernels, unit_part(): pl.pallas_call(functools.partial(gate_kernel, begin), in_specs=[hbm(), hb...  14.5 us
    all_to_all x2, starting transfers between devices, all_to_all(): return lax.all_to_all(x, axes, split_axis=0, concat_axis=0, tiled=True)  12.1 us
    all_to_all x2, waiting for transfers between devices, all_to_all(): return lax.all_to_all(x, axes, split_axis=0, concat_axis=0, tiled=True)  2.17 us
  transfers between devices with their start and end apart: 4, of which 4 were waited for; matrix products, arithmetic and copies ran while one was open for 0% of the time, Pallas kernels for 15%

profile of v2, /device:TPU:0, one launch (start us, length us, event | category | flops | bytes accessed | tf_op | source)
XLA Modules:
  0.0 97.1 jit_solution(5601937716666017764)
XLA Ops:
  0.6 14.6 %head.1 = (bf16[8,256,2048]{2,1,0:T(8,128)(2,1)}, bf16[8,256,2048]{2,1,0:T(8,128)(2,1)}, f32[256,128]{1,0:T(8,128)}, s32[128]{0:T(128)}, s32[128]{0:T(128)}) custom-call(s32[128]{0:T(128)} %bitcast.33, s32[128]{0:T(128)} %bitcast.34, s32[128]{0:T(128)} %local_s.1, bf16[16384,256]{1,0:T(8,128)(2,1)} %feat_h.3, bf16[256,256]{1,0:T(8,128)(2,1)} %win_r.1, ...), custom_call_target="tpu_custom_call" | custom-call | tf_op jit(solution)/shard_map/head/pallas_call | solution.py:359
  15.2 7.3 %all-to-all-start = ((f32[32,8,128]{2,1,0:T(8,128)}), f32[32,8,128]{2,1,0:T(8,128)S(1)}, u32[]{:S(2)}, u32[]{:S(2)}) async-start(f32[32,8,128]{2,1,0:T(8,128)} %bitcast.31), calls=%async_computation | async-start | bytes 262144 | tf_op jit(solution)/shard_map/all_to_all | solution.py:333
  22.6 0.0 copy-start.1
  22.6 0.0 copy-start.2
  22.6 7.3 %gate.2 = (bf16[8,256,2048]{2,1,0:T(8,128)(2,1)}, f32[8,128]{1,0:T(8,128)}) custom-call(bf16[8,256,2048]{2,1,0:T(8,128)(2,1)} %get-tuple-element.24.refs_0_.act1_h, bf16[8,256,2048]{2,1,0:T(8,128)(2,1)} %get-tuple-element.25.refs_1_.act2_h, bf16[256,256]{1,0:T(8,128)(2,1)} %wmid_r.3, f32[1,256]{1,0:T(1,128)} %bitcast.22), custom_call_target="tpu_custom_call" | custom-call | flops 1073741824 | bytes 12582912 | tf_op jit(solution)/shard_map/gate/pallas_call | solution.py:388
  29.9 1.1 %all-to-all-done = f32[32,8,128]{2,1,0:T(8,128)S(1)} async-done(((f32[32,8,128]{2,1,0:T(8,128)}), f32[32,8,128]{2,1,0:T(8,128)S(1)}, u32[]{:S(2)}, u32[]{:S(2)}) %all-to-all-start) | async-done | bytes 131104 | tf_op jit(solution)/shard_map/all_to_all | solution.py:333
  31.0 0.0 copy-done.1
  31.0 0.0 copy-done.2
  31.0 0.0 copy-start.5
  31.0 0.7 copy-done.5
  31.6 1.2 %coarse.1 = (f32[64,128]{1,0:T(8,128)}, f32[256,128]{1,0:T(8,128)}) custom-call(f32[256,128]{1,0:T(8,128)S(1)} %bitcast.19, f32[64,128]{1,0:T(8,128)S(1)} %copy-done.1, s32[64,128]{1,0:T(8,128)S(1)} %copy-done.2, f32[8,128]{1,0:T(8,128)S(1)} %copy-done.5), custom_call_target="tpu_custom_call" | custom-call | tf_op jit(solution)/shard_map/coarse/pallas_call | solution.py:414
  32.8 4.8 %all-to-all-start.1 = ((f32[32,8,128]{2,1,0:T(8,128)}), f32[32,8,128]{2,1,0:T(8,128)S(1)}, u32[]{:S(2)}, u32[]{:S(2)}) async-start(f32[32,8,128]{2,1,0:T(8,128)} %bitcast.9), calls=%async_computation.1 | async-start | bytes 262144 | tf_op jit(solution)/shard_map/all_to_all | solution.py:333
  37.6 7.3 %gate.3 = (bf16[8,256,2048]{2,1,0:T(8,128)(2,1)}, f32[8,128]{1,0:T(8,128)}) custom-call(bf16[8,256,2048]{2,1,0:T(8,128)(2,1)} %get-tuple-element.24.refs_0_.act1_h, bf16[8,256,2048]{2,1,0:T(8,128)(2,1)} %get-tuple-element.25.refs_1_.act2_h, bf16[256,256]{1,0:T(8,128)(2,1)} %wmid_r.3, f32[1,256]{1,0:T(1,128)} %bitcast.23, ...), custom_call_target="tpu_custom_call", output_to_operand_aliasing={{0}: (4, {})} | custom-call | flops 1073741824 | bytes 12582912 | tf_op jit(solution)/shard_map/gate/pallas_call | solution.py:388
  44.9 1.1 %all-to-all-done.1 = f32[32,8,128]{2,1,0:T(8,128)S(1)} async-done(((f32[32,8,128]{2,1,0:T(8,128)}), f32[32,8,128]{2,1,0:T(8,128)S(1)}, u32[]{:S(2)}, u32[]{:S(2)}) %all-to-all-start.1) | async-done | bytes 131104 | tf_op jit(solution)/shard_map/all_to_all | solution.py:333
  46.0 0.0 copy-start.6
  46.0 0.7 copy-done.6
  46.6 0.0 copy-start
  46.6 0.0 copy-start.3
  46.6 14.7 %back.1 = (f32[528,128]{1,0:T(8,128)}, f32[528,128]{1,0:T(8,128)}) custom-call(s32[128]{0:T(128)} %get-tuple-element.28.rows_s, s32[128]{0:T(128)} %get-tuple-element.29.inv_s, s32[1]{0:T(128)} %bitcast.8.core_s, f32[256,128]{1,0:T(8,128)} %bitcast.29, bf16[128,64,128]{2,1,0:T(8,128)(2,1)} %bitcast.28, bf16[16384,256]{1,0:T(8,128)(2,1)} %feat_h.3, ...), custom_call_target="tpu_custom_call" | custom-call | tf_op jit(solution)/shard_map/back/pallas_call | solution.py:432
  61.3 0.1 collective-permute-start
  61.4 1.7 %collective-permute-done = f32[16,1,4224]{2,1,0:T(1,128)S(1)} collective-permute-done((f32[16,1,4224]{2,1,0:T(1,128)}, f32[16,1,4224]{2,1,0:T(1,128)S(1)}, u32[]{:S(2)}, u32[]{:S(2)}) %collective-permute-start) | collective-permute-done | bytes 270368 | tf_op jit(solution)/shard_map/ppermute | solution.py:453
  63.1 1.5 %add.3 = f32[16,1,4224]{2,1,0:T(1,128)S(1)} add(f32[16,1,4224]{2,1,0:T(1,128)} %bitcast.30, f32[16,1,4224]{2,1,0:T(1,128)S(1)} %collective-permute-done) | non-fusion elementwise | flops 67584 | bytes 811008 | tf_op jit(solution)/shard_map/add | solution.py:453
  64.6 16.6 %all_to_all.20 = f32[16,1,4224]{2,1,0:T(1,128)S(1)} all-to-all(f32[16,1,4224]{2,1,0:T(1,128)S(1)} %add.3), channel_id=1, replica_groups=mesh['chip'=4,'core'=2,'coarse'=4] {'chip','coarse'}, dimensions={0} | all-to-all | bytes 540672 | tf_op jit(solution)/shard_map/all_to_all | solution.py:333
  81.3 0.2 reduce_sum.9
  81.5 0.1 broadcast_in_dim.22
  81.6 13.0 %all_to_all.21 = f32[16,1,4224]{2,1,0:T(1,128)S(1)} all-to-all(f32[16,1,4224]{2,1,0:T(1,128)S(1)} %broadcast_in_dim.22), channel_id=1, replica_groups=mesh['chip'=4,'core'=2,'coarse'=4] {'chip','coarse'}, dimensions={0} | all-to-all | bytes 540672 | tf_op jit(solution)/shard_map/all_to_all | solution.py:333
  94.6 0.0 collective-permute-start.1
  94.6 1.5 %collective-permute-done.1 = f32[16,1,4224]{2,1,0:T(1,128)S(1)} collective-permute-done((f32[16,1,4224]{2,1,0:T(1,128)S(1)}, f32[16,1,4224]{2,1,0:T(1,128)S(1)}, u32[]{:S(2)}, u32[]{:S(2)}) %collective-permute-start.1) | collective-permute-done | bytes 270368 | tf_op jit(solution)/shard_map/ppermute | solution.py:456
  96.2 0.0 copy-done
  96.2 0.0 copy-done.3
  96.2 0.0 copy-done.4
  96.2 0.9 last.1
  (1 shorter events, 0.0 us)
Async XLA Ops:
  15.2 15.7 %all-to-all-start = ((f32[32,8,128]{2,1,0:T(8,128)}), f32[32,8,128]{2,1,0:T(8,128)S(1)}, u32[]{:S(2)}, u32[]{:S(2)}) async-start(f32[32,8,128]{2,1,0:T(8,128)} %bitcast.31), calls=%async_computation | async-start | bytes 262144 | tf_op jit(solution)/shard_map/all_to_all | solution.py:333
  22.6 8.4 %copy-start.1 = (f32[64,128]{1,0:T(8,128)S(1)}, f32[64,128]{1,0:T(8,128)}, u32[]{:S(2)}) copy-start(f32[64,128]{1,0:T(8,128)} %ref_r.1) | copy-start | bytes 98308
  22.6 8.4 %copy-start.2 = (s32[64,128]{1,0:T(8,128)S(1)}, s32[64,128]{1,0:T(8,128)}, u32[]{:S(2)}) copy-start(s32[64,128]{1,0:T(8,128)} %valid_r.1) | copy-start | bytes 98308
  31.0 0.7 copy-start.5
  32.8 13.2 %all-to-all-start.1 = ((f32[32,8,128]{2,1,0:T(8,128)}), f32[32,8,128]{2,1,0:T(8,128)S(1)}, u32[]{:S(2)}, u32[]{:S(2)}) async-start(f32[32,8,128]{2,1,0:T(8,128)} %bitcast.9), calls=%async_computation.1 | async-start | bytes 262144 | tf_op jit(solution)/shard_map/all_to_all | solution.py:333
  46.0 0.7 copy-start.6
  46.6 49.6 %copy-start = (bf16[256,256]{1,0:T(8,128)(2,1)S(1)}, bf16[256,256]{1,0:T(8,128)(2,1)}, u32[]{:S(2)}) copy-start(bf16[256,256]{1,0:T(8,128)(2,1)} %wmid_r.3) | copy-start | bytes 393220
  46.6 49.6 %copy-start.3 = (f32[256]{0:T(256)S(1)}, f32[256]{0:T(256)}, u32[]{:S(2)}) copy-start(f32[256]{0:T(256)} %param.17) | copy-start | bytes 3076
  46.6 49.6 %copy-start.4 = (f32[256]{0:T(256)S(1)}, f32[256]{0:T(256)}, u32[]{:S(2)}) copy-start(f32[256]{0:T(256)} %param.16) | copy-start | bytes 3076
  61.3 1.8 %collective-permute-start = (f32[16,1,4224]{2,1,0:T(1,128)}, f32[16,1,4224]{2,1,0:T(1,128)S(1)}, u32[]{:S(2)}, u32[]{:S(2)}) collective-permute-start(f32[16,1,4224]{2,1,0:T(1,128)} %bitcast.35), channel_id=1, source_target_pairs={{0,4},{4,0},{1,5},{5,1},{2,6},{6,2},{3,7},{7,3},{8,12},{12,8},{9,1... | collective-permute-start | bytes 811016 | tf_op jit(solution)/shard_map/ppermute | solution.py:453
  94.6 1.5 %collective-permute-start.1 = (f32[16,1,4224]{2,1,0:T(1,128)S(1)}, f32[16,1,4224]{2,1,0:T(1,128)S(1)}, u32[]{:S(2)}, u32[]{:S(2)}) collective-permute-start(f32[16,1,4224]{2,1,0:T(1,128)S(1)} %all_to_all.21), channel_id=1, source_target_pairs={{0,4},{4,0},{1,5},{5,1},{2,6},{6,2},{3,7},{7,3},{8,12},{12,8},{9,1... | collective-permute-start | bytes 811016 | tf_op jit(solution)/shard_map/ppermute | solution.py:456

commit v3 on v2

--- a/solution.py
+++ b/solution.py
@@ -13,6 +13,7 @@
 CHIPS = ("chip", "coarse")
 F32 = jnp.float32
 BF16 = jnp.bfloat16
+F8 = jnp.float8_e4m3fn
 NT = (((1,), (1,)), ((), ()))
 NN = (((1,), (0,)), ((), ()))
 
@@ -129,7 +130,8 @@
         if 0 <= i - 1 < count:
             here = slice((i - 1) * chunk, i * chunk)
             pre2 = dot(wmidT[...], first.pop(i - 1)) + widen(b2[...], chunk)
-            act2_r[:, here] = pre2.astype(BF16)
+            on = pre2.astype(BF16) > 0
+            act2_r[:, here] = jnp.where(on, jnp.ones((), BF16), jnp.zeros((), BF16)).astype(F8)
             kept = jnp.maximum(pre2, 0.0) * widen(wo[...], chunk)
             preds[i - 1] = jnp.sum(kept, axis=0, keepdims=True)
         if i >= 2:
@@ -148,34 +150,26 @@
 
 
 def gate_kernel(begin, *refs):
-    act1_h, act2_h, wmid_r, wout_r = refs[:4]
-    unit_h, token_r, act1_v, act2_v, unit_v, mixed, sem_in, sem_out = refs[-8:]
+    act2_h, wmid_r, wout_r = refs[:3]
+    unit_h, act2_v, unit_v, mixed, sem_in, sem_out = refs[-6:]
     count = unit_v.shape[0]
 
-    def loads(i):
-        return [
-            pltpu.make_async_copy(src.at[begin + i], dst.at[i], sem_in.at[n, i])
-            for n, (src, dst) in enumerate(((act2_h, act2_v), (act1_h, act1_v)))
-        ]
+    def load(i):
+        return pltpu.make_async_copy(act2_h.at[begin + i], act2_v.at[i], sem_in.at[i])
 
     def store(i):
         return pltpu.make_async_copy(unit_v.at[i], unit_h.at[begin + i], sem_out.at[i])
 
     for i in range(count):
-        for copy in loads(i):
-            copy.start()
+        load(i).start()
     mixed[...] = (wmid_r[...].astype(F32) * wout_r[...]).astype(BF16)
-    token_r[...] = jnp.zeros_like(token_r)
 
     def one(i, carry):
-        for copy in loads(i):
-            copy.wait()
+        load(i).wait()
         for at in range(0, act2_v.shape[2], 256):
             here = slice(at, at + 256)
-            on = act2_v[i, :, here] > 0
-            mask = jnp.where(on, jnp.ones((), BF16), jnp.zeros((), BF16))
-            unit = dot(mixed[...], mask).astype(BF16)
-            unit_v[i, :, here] = jnp.where(act1_v[i, :, here] > 0, unit, jnp.zeros((), BF16))
+            mask = act2_v[i, :, here].astype(BF16)
+            unit_v[i, :, here] = dot(mixed[...], mask).astype(BF16)
         store(i).start()
         return carry
 
@@ -184,7 +178,7 @@
         store(i).wait()
 
 
-def coarse_kernel(scale, recv_r, ref_r, valid_r, token_r, cp_r, back_r):
+def coarse_kernel(scale, recv_r, ref_r, valid_r, unit_h, cp_r, back_r):
     cells, cb = ref_r.shape
     recv = recv_r[...]
     lane = lax.broadcasted_iota(jnp.int32, recv.shape, 1)
@@ -248,8 +242,14 @@
             grad = jnp.concatenate(
                 [grads[first + b:first + b + 1] for b in range(per_chunk)], axis=1)
             short = jnp.broadcast_to(grad.astype(BF16), (hidden, chunk))
-            gated_s[:, here] = jnp.where(act2_v[step, :, here] > 0, short, jnp.zeros((), BF16))
-            low1_s[:, here] = (unit_v[step, :, here].astype(F32) * grad).astype(BF16)
+            gated_s[:, here] = act2_v[step, :, here].astype(BF16) * short
+            low1 = unit_v[step, :, here] * short
+            low1 = jnp.where(act1_v[step, :, here] > 0, low1, jnp.zeros((), BF16))
+            low1_s[:, here] = low1
+            total = low1[:, 0:pix].astype(F32)
+            for b in range(1, per_chunk):
+                total = total + low1[:, b * pix:(b + 1) * pix].astype(F32)
+            acc_bi[...] += total
 
         def gather(i):
             here = slice(i * chunk, (i + 1) * chunk)
@@ -257,7 +257,6 @@
             lhs = jnp.concatenate([act1_v[step, :, here], ones], axis=0)
             acc_mid[...] += dot(lhs, gated_s[:, here], NT)
             acc_in[...] += dot(low1_s[:, here], feat_v[step, here, :])
-            acc_bi[...] += dot(ones, low1_s[:, here], NT)
 
         count = tile // chunk
         scale(0)
@@ -273,7 +272,9 @@
 
     width = acc_mid.shape[1]
     first = core_s[0] == 0
-    halves = ((acc_mid, acc_mid[hidden:hidden + 8, :]), (acc_in, acc_bi[0:8, :]))
+    row_bi = jnp.sum(acc_bi[...].T, axis=0, keepdims=True)
+    tail_in = jnp.concatenate([row_bi, jnp.zeros((7, width), F32)], axis=0)
+    halves = ((acc_mid, acc_mid[hidden:hidden + 8, :]), (acc_in, tail_in))
     for n, (acc, tail) in enumerate(halves):
         mine = first if n == 0 else jnp.logical_not(first)
         for out, chosen in ((keep_r, mine), (give_r, jnp.logical_not(mine))):
@@ -354,20 +355,22 @@
     row = lambda v: v[None, :]
 
     act_shape = jax.ShapeDtypeStruct((steps, hidden, tile), BF16)
+    mask_shape = jax.ShapeDtypeStruct((steps, hidden, tile), F8)
     act_v = pltpu.VMEM((steps, hidden, tile), BF16)
+    mask_v = pltpu.VMEM((steps, hidden, tile), F8)
     feat_v = pltpu.VMEM((steps, tile, chans), BF16)
     act1, act2, send, rows, inv = pl.pallas_call(
-        functools.partial(head_kernel, devices, cap, chunk),
+        functools.partial(head_kernel, devices, cap, 2 * chunk),
         in_specs=[smem()] * 3 + [hbm()] + [vmem()] * 6,
         out_specs=[hbm(), hbm(), vmem(), smem(), smem()],
         out_shape=[
-            act_shape, act_shape,
+            act_shape, mask_shape,
             jax.ShapeDtypeStruct((slots, 2 * cells), F32),
             jax.ShapeDtypeStruct((blocks,), jnp.int32),
             jax.ShapeDtypeStruct((blocks,), jnp.int32),
         ],
         scratch_shapes=[
-            feat_v, act_v, act_v,
+            feat_v, act_v, mask_v,
             pltpu.VMEM((hidden, chans), BF16),
             pltpu.VMEM((hidden, hidden), BF16),
             pltpu.VMEM((hidden, pix), F32),
@@ -387,43 +390,43 @@
         part_v = pltpu.VMEM((count, hidden, tile), BF16)
         return pl.pallas_call(
             functools.partial(gate_kernel, begin),
-            in_specs=[hbm(), hbm(), vmem(), vmem()] + [hbm()] * len(after),
-            out_specs=[hbm(), vmem()],
-            out_shape=[act_shape, jax.ShapeDtypeStruct((8, 128), F32)],
+            in_specs=[hbm(), vmem(), vmem()] + [hbm()] * len(after),
+            out_specs=hbm(),
+            out_shape=act_shape,
             scratch_shapes=[
-                part_v, part_v, part_v,
+                pltpu.VMEM((count, hidden, tile), F8), part_v,
                 pltpu.VMEM((hidden, hidden), BF16),
-                pltpu.SemaphoreType.DMA((2, count)),
+                pltpu.SemaphoreType.DMA((count,)),
                 pltpu.SemaphoreType.DMA((count,)),
             ],
-            input_output_aliases={4: 0} if after else {},
+            input_output_aliases={3: 0} if after else {},
             compiler_params=limit(58),
             cost_estimate=pl.CostEstimate(
                 flops=2 * hidden * hidden * tile * count,
-                bytes_accessed=6 * hidden * tile * count,
+                bytes_accessed=4 * hidden * tile * count,
                 transcendentals=0,
             ),
             name="gate",
-        )(act1, act2, weight_mid, row(weight_out), *after)
-
-    unit, token = unit_part(0, steps // 2)
+        )(act2, weight_mid, row(weight_out), *after)
+
+    unit = unit_part(0, steps // 2)
 
     recv = all_to_all(send.reshape(devices, cap, 2 * cells), ALL).reshape(slots, 2 * cells)
 
     scale = 1.0 / math.sqrt(blocks * devices * pix)
     coarse_pred, back = pl.pallas_call(
         functools.partial(coarse_kernel, scale),
-        in_specs=[vmem()] * 4,
+        in_specs=[vmem()] * 3 + [hbm()],
         out_specs=[vmem()] * 2,
         out_shape=[
             jax.ShapeDtypeStruct((cells, cb), F32),
             jax.ShapeDtypeStruct((slots, 2 * cells), F32),
         ],
-        compiler_params=limit(4),
+        compiler_params=limit(48),
         name="coarse",
-    )(recv, reference_map, valid_mask, token)
-
-    unit, _ = unit_part(steps // 2, steps - steps // 2, unit, back)
+    )(recv, reference_map, valid_mask, unit)
+
+    unit = unit_part(steps // 2, steps - steps // 2, unit, back)
     returned = all_to_all(back.reshape(devices, cap, 2 * cells), ALL).reshape(slots, 2 * cells)
 
     half_rows = (hidden + 8) * (chans // 128)
@@ -435,16 +438,16 @@
         out_specs=[vmem(), vmem()],
         out_shape=[half_shape, half_shape],
         scratch_shapes=[
-            feat_v, act_v, act_v, act_v,
+            feat_v, act_v, mask_v, act_v,
             pltpu.VMEM((tile // pix, pix), F32),
             pltpu.VMEM((hidden, tile), BF16),
             pltpu.VMEM((hidden, tile), BF16),
             pltpu.VMEM((hidden + 16, hidden), F32),
             pltpu.VMEM((hidden, chans), F32),
-            pltpu.VMEM((16, hidden), F32),
+            pltpu.VMEM((hidden, pix), F32),
             pltpu.SemaphoreType.DMA((4, steps)),
         ],
-        compiler_params=limit(58),
+        compiler_params=limit(48),
         name="back",
     )(rows, inv, core, returned, warp, features, act1, act2, unit)
 

time: 97.5 us -> 85.8 us (0.88)
  Pallas kernels: 45.9 us -> 36.6 us
  waiting for transfers between devices: 5.46 us -> 10.1 us
  blocking collectives: 29.6 us -> 27.3 us
  starting transfers between devices: 12.2 us -> 9.98 us
  local copies, waits for them, and re-layouts: 1.51 us -> 0.19 us
  other arithmetic: 1.68 us -> 0.45 us
    pallas_call x3, Pallas kernels: 29.1 us -> 23.2 us  [the longest x1 13.5 us: shards(): pl.pallas_call(functools.partial(head_kernel, devices, cap, 2 * chunk), i...]
    all_to_all x2, waiting for transfers between devices: 2.17 us -> 6.99 us  [all_to_all(): return lax.all_to_all(x, axes, split_axis=0, concat_axis=0, tiled=True)]
    pallas_call x1, Pallas kernels: 14.7 us -> 11.3 us  [shards(): pl.pallas_call(functools.partial(back_kernel, chunk), in_specs=[smem()] *...]
    all_to_all x2, blocking collectives: 29.6 us -> 27.3 us  [all_to_all(): return lax.all_to_all(x, axes, split_axis=0, concat_axis=0, tiled=True)]
    all_to_all x2, starting transfers between devices: 12.1 us -> 9.91 us  [all_to_all(): return lax.all_to_all(x, axes, split_axis=0, concat_axis=0, tiled=True)]
    unnamed x14 -> x16, local copies, waits for them, and re-layouts: 1.37 us -> 0.05 us
    add x1, other arithmetic: 1.51 us -> 0.28 us  [shards(): keep.reshape(chips, 1, run)]
  transfers between devices with their start and end apart: 4 -> 4, of which waited for: 4 -> 4; matrix products, arithmetic and copies ran while one was open for 0% -> 0% of each run, Pallas kernels for 15% -> 11%
where the time goes in v3:
time: 85.8 us; the launch traced here: 85.4 us
  Pallas kernels  36.6 us (43%)
  blocking collectives  27.3 us (32%)
  waiting for transfers between devices  10.1 us (12%)
  starting transfers between devices  9.98 us (12%)
    all_to_all x2, blocking collectives, all_to_all(): return lax.all_to_all(x, axes, split_axis=0, concat_axis=0, tiled=True)  27.3 us
    pallas_call x1, Pallas kernels, shards(): pl.pallas_call(functools.partial(head_kernel, devices, cap, 2 * chunk), i...  13.5 us
    pallas_call x1, Pallas kernels, shards(): pl.pallas_call(functools.partial(back_kernel, chunk), in_specs=[smem()] *...  11.3 us
    all_to_all x2, starting transfers between devices, all_to_all(): return lax.all_to_all(x, axes, split_axis=0, concat_axis=0, tiled=True)  9.91 us
    pallas_call x2, Pallas kernels, unit_part(): pl.pallas_call(functools.partial(gate_kernel, begin), in_specs=[hbm(), vm...  9.71 us
    all_to_all x2, waiting for transfers between devices, all_to_all(): return lax.all_to_all(x, axes, split_axis=0, concat_axis=0, tiled=True)  6.99 us
  transfers between devices with their start and end apart: 4, of which 4 were waited for; matrix products, arithmetic and copies ran while one was open for 0% of the time, Pallas kernels for 11%

profile of v3, /device:TPU:0, one launch (start us, length us, event | category | flops | bytes accessed | tf_op | source)
XLA Modules:
  0.0 85.4 jit_solution(14699301191783927645)
XLA Ops:
  0.6 13.5 %head.1 = (bf16[8,256,2048]{2,1,0:T(8,128)(2,1)}, f8e4m3fn[8,256,2048]{2,1,0:T(32,128)(4,1)}, f32[256,128]{1,0:T(8,128)}, s32[128]{0:T(128)}, s32[128]{0:T(128)}) custom-call(s32[128]{0:T(128)} %bitcast.34, s32[128]{0:T(128)} %bitcast.35, s32[128]{0:T(128)} %local_s.1, bf16[16384,256]{1,0:T(8,128)(2,1)} %feat_h.3, bf16[256,256]{1,0:T(8,128)(2,1)} %win_r.1, ...), custom_call_target="tpu_custom_call" | custom-call | tf_op jit(solution)/shard_map/head/pallas_call | solution.py:362
  14.1 0.0 copy-start.2
  14.2 0.0 copy-start.3
  14.2 7.3 %all-to-all-start = ((f32[32,8,128]{2,1,0:T(8,128)}), f32[32,8,128]{2,1,0:T(8,128)S(1)}, u32[]{:S(2)}, u32[]{:S(2)}) async-start(f32[32,8,128]{2,1,0:T(8,128)} %bitcast.32), calls=%async_computation | async-start | bytes 262144 | tf_op jit(solution)/shard_map/all_to_all | solution.py:334
  21.5 4.8 %gate.2.unit_h.refs_3_ = bf16[8,256,2048]{2,1,0:T(8,128)(2,1)} custom-call(f8e4m3fn[8,256,2048]{2,1,0:T(32,128)(4,1)} %get-tuple-element.21.refs_0_.act2_h, bf16[256,256]{1,0:T(8,128)(2,1)} %wmid_r.3, f32[1,256]{1,0:T(1,128)} %bitcast.26), custom_call_target="tpu_custom_call" | custom-call | flops 1073741824 | bytes 8388608 | tf_op jit(solution)/shard_map/gate/pallas_call | solution.py:391
  26.3 3.6 %all-to-all-done = f32[32,8,128]{2,1,0:T(8,128)S(1)} async-done(((f32[32,8,128]{2,1,0:T(8,128)}), f32[32,8,128]{2,1,0:T(8,128)S(1)}, u32[]{:S(2)}, u32[]{:S(2)}) %all-to-all-start) | async-done | bytes 131104 | tf_op jit(solution)/shard_map/all_to_all | solution.py:334
  29.9 0.0 copy-done.2
  29.9 0.0 copy-done.3
  29.9 1.2 %coarse.1 = (f32[64,128]{1,0:T(8,128)}, f32[256,128]{1,0:T(8,128)}) custom-call(f32[256,128]{1,0:T(8,128)S(1)} %bitcast.22, f32[64,128]{1,0:T(8,128)S(1)} %copy-done.2, s32[64,128]{1,0:T(8,128)S(1)} %copy-done.3, bf16[8,256,2048]{2,1,0:T(8,128)(2,1)} %gate.2.unit_h.refs_3_), custom_call_target="tpu_custom_call" | custom-call | tf_op jit(solution)/shard_map/coarse/pallas_call | solution.py:417
  31.1 2.6 %all-to-all-start.1 = ((f32[32,8,128]{2,1,0:T(8,128)}), f32[32,8,128]{2,1,0:T(8,128)S(1)}, u32[]{:S(2)}, u32[]{:S(2)}) async-start(f32[32,8,128]{2,1,0:T(8,128)} %bitcast.9), calls=%async_computation.1 | async-start | bytes 262144 | tf_op jit(solution)/shard_map/all_to_all | solution.py:334
  33.6 0.0 copy-start
  33.6 0.0 copy-start.6
  33.7 0.0 copy-start.7
  33.7 4.9 %gate.3.unit_h = bf16[8,256,2048]{2,1,0:T(8,128)(2,1)} custom-call(f8e4m3fn[8,256,2048]{2,1,0:T(32,128)(4,1)} %get-tuple-element.21.refs_0_.act2_h, bf16[256,256]{1,0:T(8,128)(2,1)} %wmid_r.3, f32[1,256]{1,0:T(1,128)} %bitcast.27, bf16[8,256,2048]{2,1,0:T(8,128)(2,1)} %gate.2.unit_h.refs_3_, ...), custom_call_target="tpu_custom_call", output_to_operand_aliasing={{}: (3, {})} | custom-call | flops 1073741824 | bytes 8388608 | tf_op jit(solution)/shard_map/gate/pallas_call | solution.py:391
  38.6 3.4 %all-to-all-done.1 = f32[32,8,128]{2,1,0:T(8,128)S(1)} async-done(((f32[32,8,128]{2,1,0:T(8,128)}), f32[32,8,128]{2,1,0:T(8,128)S(1)}, u32[]{:S(2)}, u32[]{:S(2)}) %all-to-all-start.1) | async-done | bytes 131104 | tf_op jit(solution)/shard_map/all_to_all | solution.py:334
  42.0 0.0 copy-done
  42.0 0.0 copy-done.6
  42.0 0.0 copy-done.7
  42.0 0.0 copy-start.1
  42.0 0.0 copy-start.4
  42.0 0.0 copy-start.5
  42.1 11.3 %back.1 = (f32[528,128]{1,0:T(8,128)S(1)}, f32[528,128]{1,0:T(8,128)S(1)}) custom-call(s32[128]{0:T(128)S(1)} %copy-done.6, s32[128]{0:T(128)S(1)} %copy-done.7, s32[1]{0:T(128)} %bitcast.8.core_s, f32[256,128]{1,0:T(8,128)S(1)} %bitcast.21, bf16[128,64,128]{2,1,0:T(8,128)(2,1)S(1)} %bitcast.19, bf16[16384,256]{1,0:T(8,128)(2,1)} %feat_h.3, ...), custom_call_target="tpu_custom_call" | custom-call | tf_op jit(solution)/shard_map/back/pallas_call | solution.py:435
  53.4 0.1 collective-permute-start
  53.5 1.5 %collective-permute-done = f32[16,1,4224]{2,1,0:T(1,128)S(1)} collective-permute-done((f32[16,1,4224]{2,1,0:T(1,128)S(1)}, f32[16,1,4224]{2,1,0:T(1,128)S(1)}, u32[]{:S(2)}, u32[]{:S(2)}) %collective-permute-start) | collective-permute-done | bytes 270368 | tf_op jit(solution)/shard_map/ppermute | solution.py:456
  55.0 0.3 add.3
  55.3 14.3 %all_to_all.20 = f32[16,1,4224]{2,1,0:T(1,128)S(1)} all-to-all(f32[16,1,4224]{2,1,0:T(1,128)S(1)} %add.3), channel_id=1, replica_groups=mesh['chip'=4,'core'=2,'coarse'=4] {'chip','coarse'}, dimensions={0} | all-to-all | bytes 540672 | tf_op jit(solution)/shard_map/all_to_all | solution.py:334
  69.6 0.2 reduce_sum.9
  69.8 0.1 broadcast_in_dim.22
  69.9 13.0 %all_to_all.21 = f32[16,1,4224]{2,1,0:T(1,128)S(1)} all-to-all(f32[16,1,4224]{2,1,0:T(1,128)S(1)} %broadcast_in_dim.22), channel_id=1, replica_groups=mesh['chip'=4,'core'=2,'coarse'=4] {'chip','coarse'}, dimensions={0} | all-to-all | bytes 540672 | tf_op jit(solution)/shard_map/all_to_all | solution.py:334
  82.9 0.0 collective-permute-start.1
  82.9 1.5 %collective-permute-done.1 = f32[16,1,4224]{2,1,0:T(1,128)S(1)} collective-permute-done((f32[16,1,4224]{2,1,0:T(1,128)S(1)}, f32[16,1,4224]{2,1,0:T(1,128)S(1)}, u32[]{:S(2)}, u32[]{:S(2)}) %collective-permute-start.1) | collective-permute-done | bytes 270368 | tf_op jit(solution)/shard_map/ppermute | solution.py:459
  84.5 0.9 %last.1 = (f32[256,256]{1,0:T(8,128)}, f32[1,256]{1,0:T(1,128)}, f32[256,256]{1,0:T(8,128)}, f32[1,256]{1,0:T(1,128)}, f32[1,256]{1,0:T(1,128)}) custom-call(s32[1]{0:T(128)} %bitcast.8.core_s, f32[528,128]{1,0:T(8,128)S(1)} %bitcast.20, f32[528,128]{1,0:T(8,128)S(1)} %bitcast.24, bf16[256,256]{1,0:T(8,128)(2,1)S(1)} %copy-done.1, f32[1,256]{1,0:T(1,128)S(1)} %bitcast.30, ...), custom_call_target="tpu_custom_call" | custom-call | tf_op jit(solution)/shard_map/last/pallas_call | solution.py:462
  (3 shorter events, 0.0 us)
Async XLA Ops:
  14.1 15.7 %copy-start.2 = (f32[64,128]{1,0:T(8,128)S(1)}, f32[64,128]{1,0:T(8,128)}, u32[]{:S(2)}) copy-start(f32[64,128]{1,0:T(8,128)} %ref_r.1) | copy-start | bytes 98308
  14.2 15.7 %copy-start.3 = (s32[64,128]{1,0:T(8,128)S(1)}, s32[64,128]{1,0:T(8,128)}, u32[]{:S(2)}) copy-start(s32[64,128]{1,0:T(8,128)} %valid_r.1) | copy-start | bytes 98308
  14.2 15.7 %all-to-all-start = ((f32[32,8,128]{2,1,0:T(8,128)}), f32[32,8,128]{2,1,0:T(8,128)S(1)}, u32[]{:S(2)}, u32[]{:S(2)}) async-start(f32[32,8,128]{2,1,0:T(8,128)} %bitcast.32), calls=%async_computation | async-start | bytes 262144 | tf_op jit(solution)/shard_map/all_to_all | solution.py:334
  31.1 11.0 %all-to-all-start.1 = ((f32[32,8,128]{2,1,0:T(8,128)}), f32[32,8,128]{2,1,0:T(8,128)S(1)}, u32[]{:S(2)}, u32[]{:S(2)}) async-start(f32[32,8,128]{2,1,0:T(8,128)} %bitcast.9), calls=%async_computation.1 | async-start | bytes 262144 | tf_op jit(solution)/shard_map/all_to_all | solution.py:334
  33.6 8.4 %copy-start = (bf16[128,128,64]{1,2,0:T(8,128)(2,1)S(1)}, bf16[128,128,64]{1,2,0:T(8,128)(2,1)}, u32[]{:S(2)}) copy-start(bf16[128,128,64]{1,2,0:T(8,128)(2,1)} %param.21) | copy-start | bytes 6291460
  33.6 8.4 %copy-start.6 = (s32[128]{0:T(128)S(1)}, s32[128]{0:T(128)}, u32[]{:S(2)}) copy-start(s32[128]{0:T(128)} %get-tuple-element.23.rows_s) | copy-start | bytes 1540
  33.7 8.4 %copy-start.7 = (s32[128]{0:T(128)S(1)}, s32[128]{0:T(128)}, u32[]{:S(2)}) copy-start(s32[128]{0:T(128)} %get-tuple-element.24.inv_s) | copy-start | bytes 1540
  42.0 42.5 %copy-start.1 = (bf16[256,256]{1,0:T(8,128)(2,1)S(1)}, bf16[256,256]{1,0:T(8,128)(2,1)}, u32[]{:S(2)}) copy-start(bf16[256,256]{1,0:T(8,128)(2,1)} %wmid_r.3) | copy-start | bytes 393220
  42.0 42.4 %copy-start.4 = (f32[256]{0:T(256)S(1)}, f32[256]{0:T(256)}, u32[]{:S(2)}) copy-start(f32[256]{0:T(256)} %param.17) | copy-start | bytes 3076
  42.0 42.4 %copy-start.5 = (f32[256]{0:T(256)S(1)}, f32[256]{0:T(256)}, u32[]{:S(2)}) copy-start(f32[256]{0:T(256)} %param.16) | copy-start | bytes 3076
  53.4 1.6 %collective-permute-start = (f32[16,1,4224]{2,1,0:T(1,128)S(1)}, f32[16,1,4224]{2,1,0:T(1,128)S(1)}, u32[]{:S(2)}, u32[]{:S(2)}) collective-permute-start(f32[16,1,4224]{2,1,0:T(1,128)S(1)} %bitcast.31), channel_id=1, source_target_pairs={{0,4},{4,0},{1,5},{5,1},{2,6},{6,2},{3,7},{7,3},{8,12},{12,8},{9,1... | collective-permute-start | bytes 811016 | tf_op jit(solution)/shard_map/ppermute | solution.py:456
  82.9 1.5 %collective-permute-start.1 = (f32[16,1,4224]{2,1,0:T(1,128)S(1)}, f32[16,1,4224]{2,1,0:T(1,128)S(1)}, u32[]{:S(2)}, u32[]{:S(2)}) collective-permute-start(f32[16,1,4224]{2,1,0:T(1,128)S(1)} %all_to_all.21), channel_id=1, source_target_pairs={{0,4},{4,0},{1,5},{5,1},{2,6},{6,2},{3,7},{7,3},{8,12},{12,8},{9,1... | collective-permute-start | bytes 811016 | tf_op jit(solution)/shard_map/ppermute | solution.py:459

commit v4 on v3

--- a/solution.py
+++ b/solution.py
@@ -10,7 +10,8 @@
 from jax.sharding import PartitionSpec as P
 
 ALL = ("chip", "core", "coarse")
-CHIPS = ("chip", "coarse")
+CHIPS = ("coarse", "chip")
+EXCHANGE = ("coarse", "chip", "core")
 F32 = jnp.float32
 BF16 = jnp.bfloat16
 F8 = jnp.float8_e4m3fn
@@ -45,7 +46,7 @@
 
 
 def head_kernel(
-    devices, cap, chunk,
+    devices, depth, cap, chunk,
     fine_s, owner_s, local_s,
     feat_h, win_r, bin_r, wmid_r, bmid_r, wout_r, warp_r,
     act1_h, act2_h, send_r, rows_r, inv_r,
@@ -74,7 +75,7 @@
         b1[...] = column(bin_r[...], pix)
         b2[...] = column(bmid_r[...], pix)
         wo[...] = column(wout_r[...], pix)
-        lane = lax.broadcasted_iota(jnp.int32, send_r.shape, 1)
+        lane = lax.broadcasted_iota(jnp.int32, send_r.shape, 2)
         send_r[...] = jnp.where(lane < cells, 0.0, -1.0)
         for i in range(devices):
             count_s[i] = 0
@@ -87,12 +88,12 @@
 
     prepare()
     lax.fori_loop(0, steps, functools.partial(
-        head_step, chunk, per_chunk, per_step, cap, load, stores,
+        head_step, chunk, per_chunk, per_step, (devices, depth, cap), load, stores,
         fine_s, owner_s, local_s, feat_v, act1_v, act2_v, warp_r,
         rows_r, inv_r, winT, wmidT, b1, b2, wo, part_s, count_s), 0)
 
     def place(k, c):
-        send_r[pl.ds(rows_r[k], 1), :] = part_s[pl.ds(k, 1), :]
+        send_r[rows_r[k]] = part_s[k]
         return c
 
     lax.fori_loop(0, blocks, place, 0, unroll=16)
@@ -102,7 +103,7 @@
 
 
 def head_step(
-    chunk, per_chunk, per_step, cap, load, stores,
+    chunk, per_chunk, per_step, sizes, load, stores,
     fine_s, owner_s, local_s, feat_v, act1_v, act2_v, warp_r,
     rows_r, inv_r, winT, wmidT, b1, b2, wo, part_s, count_s,
     step, carry,
@@ -117,7 +118,9 @@
         owner = owner_s[k]
         rank = count_s[owner]
         count_s[owner] = rank + 1
-        rows_r[k] = owner * cap + rank
+        devices, depth, cap = sizes
+        place = (owner % depth) * (devices // depth) + owner // depth
+        rows_r[k] = place * cap + rank
 
     count = tile // chunk
     first, preds = {}, {}
@@ -140,9 +143,9 @@
                 k = inv_r[step * per_step + (i - 2) * per_chunk + b]
                 one = jnp.broadcast_to(pred[:, b * pix:(b + 1) * pix], (8, pix))
                 part = dot(terms_by_row(one).astype(BF16), warp_r[k], NT)
-                part_s[pl.ds(k, 1), 0:cells] = jnp.sum(part, axis=0, keepdims=True)
-                tag = jnp.full((1, part_s.shape[1] - cells), local_s[k], jnp.int32).astype(F32)
-                part_s[pl.ds(k, 1), cells:] = tag
+                part_s[k, :, 0:cells] = jnp.sum(part, axis=0, keepdims=True)
+                tag = jnp.full((1, part_s.shape[2] - cells), local_s[k], jnp.int32).astype(F32)
+                part_s[k, :, cells:] = tag
 
     for copy in stores(step):
         copy.start()
@@ -360,12 +363,12 @@
     mask_v = pltpu.VMEM((steps, hidden, tile), F8)
     feat_v = pltpu.VMEM((steps, tile, chans), BF16)
     act1, act2, send, rows, inv = pl.pallas_call(
-        functools.partial(head_kernel, devices, cap, 2 * chunk),
+        functools.partial(head_kernel, devices, lax.axis_size("coarse"), cap, 2 * chunk),
         in_specs=[smem()] * 3 + [hbm()] + [vmem()] * 6,
         out_specs=[hbm(), hbm(), vmem(), smem(), smem()],
         out_shape=[
             act_shape, mask_shape,
-            jax.ShapeDtypeStruct((slots, 2 * cells), F32),
+            jax.ShapeDtypeStruct((slots, 1, 2 * cells), F32),
             jax.ShapeDtypeStruct((blocks,), jnp.int32),
             jax.ShapeDtypeStruct((blocks,), jnp.int32),
         ],
@@ -376,7 +379,7 @@
             pltpu.VMEM((hidden, pix), F32),
             pltpu.VMEM((hidden, pix), F32),
             pltpu.VMEM((hidden, pix), F32),
-            pltpu.VMEM((blocks, 2 * cells), F32),
+            pltpu.VMEM((blocks, 1, 2 * cells), F32),
             pltpu.SMEM((devices,), jnp.int32),
             pltpu.SemaphoreType.DMA((steps,)),
             pltpu.SemaphoreType.DMA((2, steps)),
@@ -411,7 +414,7 @@
 
     unit = unit_part(0, steps // 2)
 
-    recv = all_to_all(send.reshape(devices, cap, 2 * cells), ALL).reshape(slots, 2 * cells)
+    recv = all_to_all(send.reshape(devices, cap, 2 * cells), EXCHANGE).reshape(slots, 2 * cells)
 
     scale = 1.0 / math.sqrt(blocks * devices * pix)
     coarse_pred, back = pl.pallas_call(
@@ -427,7 +430,7 @@
     )(recv, reference_map, valid_mask, unit)
 
     unit = unit_part(steps // 2, steps - steps // 2, unit, back)
-    returned = all_to_all(back.reshape(devices, cap, 2 * cells), ALL).reshape(slots, 2 * cells)
+    returned = all_to_all(back.reshape(devices, cap, 2 * cells), EXCHANGE).reshape(slots, 2 * cells)
 
     half_rows = (hidden + 8) * (chans // 128)
     half_shape = jax.ShapeDtypeStruct((half_rows, 128), F32)

time: 85.8 us -> 84.9 us (0.990)
  no operation moved by 1% of the time
where the time goes in v4:
time: 84.9 us; the launch traced here: 84.5 us
  Pallas kernels  36.6 us (43%)
  blocking collectives  26.8 us (32%)
  starting transfers between devices  10.2 us (12%)
  waiting for transfers between devices  9.5 us (11%)
    all_to_all x2, blocking collectives, all_to_all(): return lax.all_to_all(x, axes, split_axis=0, concat_axis=0, tiled=True)  26.8 us
    pallas_call x1, Pallas kernels, shards(): pl.pallas_call(functools.partial(head_kernel, devices, lax.axis_size('coa...  13.5 us
    pallas_call x1, Pallas kernels, shards(): pl.pallas_call(functools.partial(back_kernel, chunk), in_specs=[smem()] *...  11.3 us
    all_to_all x2, starting transfers between devices, all_to_all(): return lax.all_to_all(x, axes, split_axis=0, concat_axis=0, tiled=True)  9.91 us
    pallas_call x2, Pallas kernels, unit_part(): pl.pallas_call(functools.partial(gate_kernel, begin), in_specs=[hbm(), vm...  9.71 us
    all_to_all x2, waiting for transfers between devices, all_to_all(): return lax.all_to_all(x, axes, split_axis=0, concat_axis=0, tiled=True)  6.64 us
  transfers between devices with their start and end apart: 4, of which 4 were waited for; matrix products, arithmetic and copies ran while one was open for 0% of the time, Pallas kernels for 11%

profile of v4, /device:TPU:0, one launch (start us, length us, event | category | flops | bytes accessed | tf_op | source)
XLA Modules:
  0.0 84.5 jit_solution(13338040736083538992)
XLA Ops:
  0.6 13.5 %head.1 = (bf16[8,256,2048]{2,1,0:T(8,128)(2,1)}, f8e4m3fn[8,256,2048]{2,1,0:T(32,128)(4,1)}, f32[256,1,128]{2,1,0:T(1,128)}, s32[128]{0:T(128)}, s32[128]{0:T(128)}) custom-call(s32[128]{0:T(128)} %bitcast.34, s32[128]{0:T(128)} %bitcast.35, s32[128]{0:T(128)} %local_s.1, bf16[16384,256]{1,0:T(8,128)(2,1)} %feat_h.3, bf16[256,256]{1,0:T(8,128)(2,1)} %win_r.1, ...), custom_call_target="tpu_custom_call" | custom-call | tf_op jit(solution)/shard_map/head/pallas_call | solution.py:365
  14.2 0.0 copy-start.2
  14.2 0.0 copy-start.3
  14.2 7.3 %all-to-all-start = ((f32[32,8,128]{2,1,0:T(8,128)}), f32[32,8,128]{2,1,0:T(8,128)S(1)}, u32[]{:S(2)}, u32[]{:S(2)}) async-start(f32[32,8,128]{2,1,0:T(8,128)} %bitcast.32), calls=%async_computation | async-start | bytes 262144 | tf_op jit(solution)/shard_map/all_to_all | solution.py:337
  21.5 4.8 %gate.2.unit_h.refs_3_ = bf16[8,256,2048]{2,1,0:T(8,128)(2,1)} custom-call(f8e4m3fn[8,256,2048]{2,1,0:T(32,128)(4,1)} %get-tuple-element.21.refs_0_.act2_h, bf16[256,256]{1,0:T(8,128)(2,1)} %wmid_r.3, f32[1,256]{1,0:T(1,128)} %bitcast.26), custom_call_target="tpu_custom_call" | custom-call | flops 1073741824 | bytes 8388608 | tf_op jit(solution)/shard_map/gate/pallas_call | solution.py:394
  26.3 3.4 %all-to-all-done = f32[32,8,128]{2,1,0:T(8,128)S(1)} async-done(((f32[32,8,128]{2,1,0:T(8,128)}), f32[32,8,128]{2,1,0:T(8,128)S(1)}, u32[]{:S(2)}, u32[]{:S(2)}) %all-to-all-start) | async-done | bytes 131104 | tf_op jit(solution)/shard_map/all_to_all | solution.py:337
  29.7 0.0 copy-done.2
  29.8 0.0 copy-done.3
  29.8 1.2 %coarse.1 = (f32[64,128]{1,0:T(8,128)}, f32[256,128]{1,0:T(8,128)}) custom-call(f32[256,128]{1,0:T(8,128)S(1)} %bitcast.22, f32[64,128]{1,0:T(8,128)S(1)} %copy-done.2, s32[64,128]{1,0:T(8,128)S(1)} %copy-done.3, bf16[8,256,2048]{2,1,0:T(8,128)(2,1)} %gate.2.unit_h.refs_3_), custom_call_target="tpu_custom_call" | custom-call | tf_op jit(solution)/shard_map/coarse/pallas_call | solution.py:420
  30.9 2.6 %all-to-all-start.1 = ((f32[32,8,128]{2,1,0:T(8,128)}), f32[32,8,128]{2,1,0:T(8,128)S(1)}, u32[]{:S(2)}, u32[]{:S(2)}) async-start(f32[32,8,128]{2,1,0:T(8,128)} %bitcast.9), calls=%async_computation.1 | async-start | bytes 262144 | tf_op jit(solution)/shard_map/all_to_all | solution.py:337
  33.5 0.0 copy-start
  33.5 0.0 copy-start.6
  33.5 0.0 copy-start.7
  33.5 4.9 %gate.3.unit_h = bf16[8,256,2048]{2,1,0:T(8,128)(2,1)} custom-call(f8e4m3fn[8,256,2048]{2,1,0:T(32,128)(4,1)} %get-tuple-element.21.refs_0_.act2_h, bf16[256,256]{1,0:T(8,128)(2,1)} %wmid_r.3, f32[1,256]{1,0:T(1,128)} %bitcast.27, bf16[8,256,2048]{2,1,0:T(8,128)(2,1)} %gate.2.unit_h.refs_3_, ...), custom_call_target="tpu_custom_call", output_to_operand_aliasing={{}: (3, {})} | custom-call | flops 1073741824 | bytes 8388608 | tf_op jit(solution)/shard_map/gate/pallas_call | solution.py:394
  38.5 3.2 %all-to-all-done.1 = f32[32,8,128]{2,1,0:T(8,128)S(1)} async-done(((f32[32,8,128]{2,1,0:T(8,128)}), f32[32,8,128]{2,1,0:T(8,128)S(1)}, u32[]{:S(2)}, u32[]{:S(2)}) %all-to-all-start.1) | async-done | bytes 131104 | tf_op jit(solution)/shard_map/all_to_all | solution.py:337
  41.7 0.0 copy-done
  41.7 0.0 copy-start.1
  41.7 0.0 copy-start.4
  41.7 0.0 copy-start.5
  41.7 11.3 %back.1 = (f32[528,128]{1,0:T(8,128)S(1)}, f32[528,128]{1,0:T(8,128)S(1)}) custom-call(s32[128]{0:T(128)S(1)} %copy-done.6, s32[128]{0:T(128)S(1)} %copy-done.7, s32[1]{0:T(128)} %bitcast.8.core_s, f32[256,128]{1,0:T(8,128)S(1)} %bitcast.21, bf16[128,64,128]{2,1,0:T(8,128)(2,1)S(1)} %bitcast.19, bf16[16384,256]{1,0:T(8,128)(2,1)} %feat_h.3, ...), custom_call_target="tpu_custom_call" | custom-call | tf_op jit(solution)/shard_map/back/pallas_call | solution.py:438
  53.1 0.3 collective-permute-start
  53.4 1.3 %collective-permute-done = f32[16,1,4224]{2,1,0:T(1,128)S(1)} collective-permute-done((f32[16,1,4224]{2,1,0:T(1,128)S(1)}, f32[16,1,4224]{2,1,0:T(1,128)S(1)}, u32[]{:S(2)}, u32[]{:S(2)}) %collective-permute-start) | collective-permute-done | bytes 270368 | tf_op jit(solution)/shard_map/ppermute | solution.py:459
  54.7 0.3 add.3
  55.0 13.8 %all_to_all.20 = f32[16,1,4224]{2,1,0:T(1,128)S(1)} all-to-all(f32[16,1,4224]{2,1,0:T(1,128)S(1)} %add.3), channel_id=1, replica_groups=mesh['chip'=4,'core'=2,'coarse'=4] {'coarse','chip'}, dimensions={0} | all-to-all | bytes 540672 | tf_op jit(solution)/shard_map/all_to_all | solution.py:337
  68.7 0.2 reduce_sum.9
  68.9 0.1 broadcast_in_dim.22
  69.1 13.0 %all_to_all.21 = f32[16,1,4224]{2,1,0:T(1,128)S(1)} all-to-all(f32[16,1,4224]{2,1,0:T(1,128)S(1)} %broadcast_in_dim.22), channel_id=1, replica_groups=mesh['chip'=4,'core'=2,'coarse'=4] {'coarse','chip'}, dimensions={0} | all-to-all | bytes 540672 | tf_op jit(solution)/shard_map/all_to_all | solution.py:337
  82.0 0.0 collective-permute-start.1
  82.0 1.5 %collective-permute-done.1 = f32[16,1,4224]{2,1,0:T(1,128)S(1)} collective-permute-done((f32[16,1,4224]{2,1,0:T(1,128)S(1)}, f32[16,1,4224]{2,1,0:T(1,128)S(1)}, u32[]{:S(2)}, u32[]{:S(2)}) %collective-permute-start.1) | collective-permute-done | bytes 270368 | tf_op jit(solution)/shard_map/ppermute | solution.py:462
  83.6 0.0 copy-done.1
  83.6 0.0 copy-done.5
  83.6 0.9 %last.1 = (f32[256,256]{1,0:T(8,128)}, f32[1,256]{1,0:T(1,128)}, f32[256,256]{1,0:T(8,128)}, f32[1,256]{1,0:T(1,128)}, f32[1,256]{1,0:T(1,128)}) custom-call(s32[1]{0:T(128)} %bitcast.8.core_s, f32[528,128]{1,0:T(8,128)S(1)} %bitcast.20, f32[528,128]{1,0:T(8,128)S(1)} %bitcast.24, bf16[256,256]{1,0:T(8,128)(2,1)S(1)} %copy-done.1, f32[1,256]{1,0:T(1,128)S(1)} %bitcast.30, ...), custom_call_target="tpu_custom_call" | custom-call | tf_op jit(solution)/shard_map/last/pallas_call | solution.py:465
  (3 shorter events, 0.0 us)
Async XLA Ops:
  14.2 15.6 %copy-start.2 = (f32[64,128]{1,0:T(8,128)S(1)}, f32[64,128]{1,0:T(8,128)}, u32[]{:S(2)}) copy-start(f32[64,128]{1,0:T(8,128)} %ref_r.1) | copy-start | bytes 98308
  14.2 15.6 %copy-start.3 = (s32[64,128]{1,0:T(8,128)S(1)}, s32[64,128]{1,0:T(8,128)}, u32[]{:S(2)}) copy-start(s32[64,128]{1,0:T(8,128)} %valid_r.1) | copy-start | bytes 98308
  14.2 15.5 %all-to-all-start = ((f32[32,8,128]{2,1,0:T(8,128)}), f32[32,8,128]{2,1,0:T(8,128)S(1)}, u32[]{:S(2)}, u32[]{:S(2)}) async-start(f32[32,8,128]{2,1,0:T(8,128)} %bitcast.32), calls=%async_computation | async-start | bytes 262144 | tf_op jit(solution)/shard_map/all_to_all | solution.py:337
  30.9 10.8 %all-to-all-start.1 = ((f32[32,8,128]{2,1,0:T(8,128)}), f32[32,8,128]{2,1,0:T(8,128)S(1)}, u32[]{:S(2)}, u32[]{:S(2)}) async-start(f32[32,8,128]{2,1,0:T(8,128)} %bitcast.9), calls=%async_computation.1 | async-start | bytes 262144 | tf_op jit(solution)/shard_map/all_to_all | solution.py:337
  33.5 8.2 %copy-start = (bf16[128,128,64]{1,2,0:T(8,128)(2,1)S(1)}, bf16[128,128,64]{1,2,0:T(8,128)(2,1)}, u32[]{:S(2)}) copy-start(bf16[128,128,64]{1,2,0:T(8,128)(2,1)} %param.21) | copy-start | bytes 6291460
  33.5 8.2 %copy-start.6 = (s32[128]{0:T(128)S(1)}, s32[128]{0:T(128)}, u32[]{:S(2)}) copy-start(s32[128]{0:T(128)} %get-tuple-element.23.rows_s) | copy-start | bytes 1540
  33.5 8.2 %copy-start.7 = (s32[128]{0:T(128)S(1)}, s32[128]{0:T(128)}, u32[]{:S(2)}) copy-start(s32[128]{0:T(128)} %get-tuple-element.24.inv_s) | copy-start | bytes 1540
  41.7 41.9 %copy-start.1 = (bf16[256,256]{1,0:T(8,128)(2,1)S(1)}, bf16[256,256]{1,0:T(8,128)(2,1)}, u32[]{:S(2)}) copy-start(bf16[256,256]{1,0:T(8,128)(2,1)} %wmid_r.3) | copy-start | bytes 393220
  41.7 41.9 %copy-start.4 = (f32[256]{0:T(256)S(1)}, f32[256]{0:T(256)}, u32[]{:S(2)}) copy-start(f32[256]{0:T(256)} %param.17) | copy-start | bytes 3076
  41.7 41.9 %copy-start.5 = (f32[256]{0:T(256)S(1)}, f32[256]{0:T(256)}, u32[]{:S(2)}) copy-start(f32[256]{0:T(256)} %param.16) | copy-start | bytes 3076
  53.1 1.6 %collective-permute-start = (f32[16,1,4224]{2,1,0:T(1,128)S(1)}, f32[16,1,4224]{2,1,0:T(1,128)S(1)}, u32[]{:S(2)}, u32[]{:S(2)}) collective-permute-start(f32[16,1,4224]{2,1,0:T(1,128)S(1)} %bitcast.31), channel_id=1, source_target_pairs={{0,4},{4,0},{1,5},{5,1},{2,6},{6,2},{3,7},{7,3},{8,12},{12,8},{9,1... | collective-permute-start | bytes 811016 | tf_op jit(solution)/shard_map/ppermute | solution.py:459
  82.0 1.5 %collective-permute-start.1 = (f32[16,1,4224]{2,1,0:T(1,128)S(1)}, f32[16,1,4224]{2,1,0:T(1,128)S(1)}, u32[]{:S(2)}, u32[]{:S(2)}) collective-permute-start(f32[16,1,4224]{2,1,0:T(1,128)S(1)} %all_to_all.21), channel_id=1, source_target_pairs={{0,4},{4,0},{1,5},{5,1},{2,6},{6,2},{3,7},{7,3},{8,12},{12,8},{9,1... | collective-permute-start | bytes 811016 | tf_op jit(solution)/shard_map/ppermute | solution.py:462
